TPU v7x, 128 devices: a whole 4x4x4 slice. The times are simulated.
128 devices in a mesh: tm: 8 (over z_hi, x), space: 16 (over z_lo, y, core).
Axes of the slice: x: 4, y: 4, z: 4 (z_hi: 2, z_lo: 2; z = z_hi * 2 + z_lo), core: 2. Of those that a mesh axis runs over, the one named last changes fastest.
Arguments:
- activations: bfloat16 [64, 32, 8, 1024], P('tm', 'space'), may hold values from -6 to 6
- in_proj: bfloat16 [1024, 2176], replicated, may hold values from -0.1875 to 0.1875
- step_proj: bfloat16 [1024, 16], replicated, may hold values from -0.1875 to 0.1875
- step_bias: float32 [16], replicated, may hold values from -2 to 0
- decay_rates: float32 [16], replicated, may hold values from 0.005 to 0.5
- conv_kernel: float32 [3, 3, 1152], replicated, may hold values from -2 to 2
- conv_bias: float32 [1152], replicated, may hold values from -3 to 3
- skip_gain: float32 [16], replicated, may hold values from 0.5 to 1.5
- norm_gain: float32 [1024], replicated, may hold values from 0.5 to 1.5
- out_proj: bfloat16 [1024, 1024], replicated, may hold values from -0.1875 to 0.1875
- out_cotangent: bfloat16 [64, 32, 8, 1024], P('tm', 'space'), may hold values from -6 to 6
Outputs:
- layer_out: bfloat16 [64, 32, 8, 1024], P('tm', 'space')
- grad_input: bfloat16 [64, 32, 8, 1024], P('tm', 'space')
- grad_in_proj: float32 [1024, 2176], P(('tm', 'space'))
- grad_step_proj: float32 [1024, 16], P(('tm', 'space'))
- grad_out_proj_t: float32 [1024, 1024], P(('tm', 'space'))
- grad_conv_kernel: float32 [3, 3, 1152], replicated
- grad_conv_bias: float32 [1152], replicated
- grad_step_bias: float32 [16], replicated
- grad_decay_rates: float32 [16], replicated
- grad_skip_gain: float32 [16], replicated
- grad_norm_gain: float32 [1024], replicated
All inputs are finite; a program needn't handle non-finite values.
Results may differ from a plain program's by a relative error of at most 0.015.
The roundings to bfloat16 on the way count: a program that leaves them out, or rounds other values in their place, can miss the bound.
Values may be sent and summed in bfloat16 or wider, within the bound.
No kernel may reach another device: no remote copies, remote signals or barrier semaphores. Data moves between devices by JAX's collectives and lax.ppermute only.
A program may use at most 192 MiB of HBM per device.

v0:
```python
import jax
import jax.numpy as jnp
from jax import lax
from jax.sharding import Mesh
from jax.sharding import PartitionSpec as P

SPACE = ("space_0", "space_1", "space_2")
TM = ("tm_0", "tm_1")
TM_SPACE = ("tm_0", "tm_1", "space_0", "space_1", "space_2")


top_precision = lax.Precision.HIGHEST
norm_eps = 1e-05


def padded_2(block, sides, width):
    for axis, dim in sides:
        count = lax.axis_size(axis)
        forward = [(i, i + 1) for i in range(count - 1)]
        backward = [(target, source) for source, target in forward]
        low = lax.ppermute(
            lax.slice_in_dim(block, block.shape[dim] - width, None, axis=dim), axis, forward
        )
        high = lax.ppermute(lax.slice_in_dim(block, 0, width, axis=dim), axis, backward)
        block = jnp.concatenate([low, block, high], axis=dim)
    return block


def side_by_side(arrays, axis, split_dim, concat_dim, along):
    widths = [a.shape[along] for a in arrays]
    both = jnp.concatenate(arrays, axis=along)
    whole = lax.all_to_all(both, axis, split_axis=split_dim, concat_axis=concat_dim, tiled=True)
    return tuple(jnp.split(whole, [sum(widths[:k]) for k in range(1, len(widths))], axis=along))


def from_behind(block, axis, distance):
    devices = range(lax.axis_size(axis))
    route = [(i - distance, i) for i in devices if i - distance in devices]
    return lax.ppermute(block, axis, route)


def split_up(array, dim, peers):
    before, after = (array.shape[:dim], array.shape[dim + 1 :])
    return jnp.moveaxis(array.reshape(*before, peers, -1, *after), dim, 0)


def scatter_pairs(array, chips, core, dim):
    sizes = (lax.axis_size(chips), lax.axis_size(core))
    parts = split_up(array, dim, sizes[0] * sizes[1])
    inside = parts.shape[1:]
    parts = parts.reshape(*sizes, *inside).swapaxes(0, 1).reshape(-1, *inside)
    parts = lax.psum_scatter(parts, core, scatter_dimension=0, tiled=True)
    return lax.psum_scatter(parts, chips, scatter_dimension=0, tiled=True)[0]


def together(arrays, axis):
    ends = [0]
    for a in arrays:
        ends.append(ends[-1] + a.size)
    total = lax.psum(jnp.concatenate([a.ravel() for a in arrays]), axis)
    return tuple((total[b:e].reshape(a.shape) for a, b, e in zip(arrays, ends, ends[1:])))


def ssd_block(heads_in, b_proj, c_proj, step_in, rate_in, gain_in, state_in):
    decay_step = step_in * rate_in
    running = jnp.cumsum(decay_step, axis=0)
    places = jnp.arange(heads_in.shape[0])
    causal = (places[:, None] >= places[None, :])[:, :, None, None]
    spread = running[:, None] - running[None, :]
    weights = jnp.where(causal, jnp.exp(-jnp.where(causal, spread, 0.0)), 0.0) * step_in[None, :]
    inner_cb = jnp.einsum("tkn,skn->tsk", c_proj, b_proj, precision=top_precision)
    intra_part = jnp.einsum(
        "tskh,skhp->tkhp", weights * inner_cb[..., None], heads_in, precision=top_precision
    )
    carried = jnp.exp(-running)[..., None] * jnp.einsum(
        "tkn,khpn->tkhp", c_proj, state_in, precision=top_precision
    )
    result = intra_part + carried + gain_in[:, None] * heads_in
    final_sum = running[-1]
    tail_weight = jnp.exp(running - final_sum[None]) * step_in
    state_out = jnp.exp(-final_sum)[..., None, None] * state_in + jnp.einsum(
        "skh,skhp,skn->khpn", tail_weight, heads_in, b_proj, precision=top_precision
    )
    return (result, state_out)


def ssd_sequence(heads_in, b_proj, c_proj, step_in, rate_in, gain_in, block_len):
    block_count = heads_in.shape[0] // block_len

    def fold_blocks(array_in):
        return array_in.reshape((block_count, block_len) + array_in.shape[1:])

    start_state = jnp.zeros(heads_in.shape[1:4] + (b_proj.shape[2],), jnp.float32)

    def advance(carry_state, pieces):
        result, carry_state = ssd_block(
            pieces[0], pieces[1], pieces[2], pieces[3], rate_in, gain_in, carry_state
        )
        return (carry_state, result)

    final_state, results = lax.scan(
        advance,
        start_state,
        (fold_blocks(heads_in), fold_blocks(b_proj), fold_blocks(c_proj), fold_blocks(step_in)),
    )
    return (results.reshape(heads_in.shape), final_state)


def gate_norm(ssd_float, gate_float, norm_gain):
    gated = ssd_float * jax.nn.silu(gate_float)
    scale_row = lax.rsqrt(jnp.mean(gated * gated, axis=-1, keepdims=True) + norm_eps)
    return gated * scale_row * norm_gain


def silu_slope(before):
    squashed = jax.nn.sigmoid(before)
    return squashed * (1.0 + before * (1.0 - squashed))


def conv_apply(padded, conv_kernel, conv_bias, row_count, col_count):
    accum = conv_kernel[0, 0] * padded[:, 0:row_count, 0:col_count]
    for row_off in range(3):
        for col_off in range(3):
            if row_off + col_off > 0:
                accum = (
                    accum
                    + conv_kernel[row_off, col_off]
                    * padded[:, row_off : row_off + row_count, col_off : col_off + col_count]
                )
    return accum + conv_bias


def conv_spread(d_before, conv_kernel):
    accum = jnp.pad(conv_kernel[0, 0] * d_before, ((0, 0), (0, 2), (0, 2), (0, 0)))
    for row_off in range(3):
        for col_off in range(3):
            if row_off + col_off > 0:
                accum = accum + jnp.pad(
                    conv_kernel[row_off, col_off] * d_before,
                    ((0, 0), (row_off, 2 - row_off), (col_off, 2 - col_off), (0, 0)),
                )
    return accum


def kernel_grad(d_before, padded, row_count, col_count):
    parts = []
    for row_off in range(3):
        for col_off in range(3):
            parts.append(
                jnp.sum(
                    d_before
                    * padded[:, row_off : row_off + row_count, col_off : col_off + col_count],
                    axis=(0, 1, 2),
                )
            )
    return jnp.stack(parts).reshape(3, 3, -1)


def on_device(
    activations,
    in_proj,
    step_proj,
    step_bias,
    decay_rates,
    conv_kernel,
    conv_bias,
    skip_gain,
    norm_gain,
    out_proj,
    out_cotangent,
):
    frame_count, row_count, col_count, model_width = activations.shape
    inner_w = out_proj.shape[0]
    head_count = step_proj.shape[1]
    head_dim = inner_w // head_count
    proj_cols = in_proj.shape[1]
    state_n = (proj_cols - 2 * inner_w) // 2
    token_count = row_count * col_count
    flat_act = activations.reshape(-1, model_width)
    projected = jnp.dot(flat_act, in_proj, preferred_element_type=jnp.float32)
    gate_z = projected[:, :inner_w].astype(jnp.bfloat16)
    mixed_in = (
        projected[:, inner_w:].astype(jnp.bfloat16).reshape(frame_count, row_count, col_count, -1)
    )
    step_raw = jnp.dot(flat_act, step_proj, preferred_element_type=jnp.float32) + step_bias
    step_sizes = jax.nn.softplus(step_raw).astype(jnp.bfloat16)
    halo_rows = padded_2(mixed_in, ((SPACE, 1),), 1)
    padded = jnp.pad(halo_rows.astype(jnp.float32), ((0, 0), (0, 0), (1, 1), (0, 0)))
    before = conv_apply(padded, conv_kernel, conv_bias, row_count, col_count)
    activated = jax.nn.silu(before).astype(jnp.bfloat16).reshape(frame_count, token_count, -1)
    steps_tok = step_sizes.reshape(frame_count, token_count, head_count)
    moved_act, moved_steps = side_by_side((activated, steps_tok), TM, 1, 0, 2)
    all_frames = moved_act.shape[0]
    few_tokens = moved_act.shape[1]
    act_float = moved_act.astype(jnp.float32)
    heads_in = act_float[..., :inner_w].reshape(all_frames, few_tokens, head_count, head_dim)
    heads_in, b_proj, c_proj = (
        heads_in,
        act_float[..., inner_w : inner_w + state_n],
        act_float[..., inner_w + state_n :],
    )

    def ssd_whole(heads_arg, b_arg, c_arg, step_arg, rate_arg, gain_arg):
        return ssd_sequence(heads_arg, b_arg, c_arg, step_arg, rate_arg, gain_arg, frame_count)

    (ssd_float, final_state), pull_back = jax.vjp(
        ssd_whole, heads_in, b_proj, c_proj, moved_steps.astype(jnp.float32), decay_rates, skip_gain
    )
    returned = lax.all_to_all(
        ssd_float.astype(jnp.bfloat16).reshape(all_frames, few_tokens, inner_w),
        TM,
        split_axis=0,
        concat_axis=1,
        tiled=True,
    )
    ssd_out = returned.reshape(frame_count * token_count, inner_w)
    normed_float, pull_norm = jax.vjp(
        gate_norm, ssd_out.astype(jnp.float32), gate_z.astype(jnp.float32), norm_gain
    )
    normed = normed_float.astype(jnp.bfloat16)
    layer_out = (
        jnp.dot(normed, out_proj, preferred_element_type=jnp.float32)
        .astype(jnp.bfloat16)
        .reshape(activations.shape)
    )
    contract_rows = (((0,), (0,)), ((), ()))
    contract_cols = (((1,), (1,)), ((), ()))
    cot_flat = out_cotangent.reshape(-1, model_width)
    d_normed = lax.dot_general(
        cot_flat, out_proj, contract_cols, preferred_element_type=jnp.float32
    )
    d_ssd, d_gate, norm_part = pull_norm(d_normed)
    d_ssd = d_ssd.astype(jnp.bfloat16)
    moved_grad = lax.all_to_all(
        d_ssd.reshape(frame_count, token_count, inner_w),
        TM,
        split_axis=1,
        concat_axis=0,
        tiled=True,
    )
    d_result = moved_grad.astype(jnp.float32).reshape(all_frames, few_tokens, head_count, head_dim)
    gradients = pull_back((d_result, jnp.zeros_like(final_state)))
    d_act_seq = jnp.concatenate(
        [gradients[0].reshape(all_frames, few_tokens, inner_w), gradients[1], gradients[2]], axis=-1
    ).astype(jnp.bfloat16)
    d_steps_seq = gradients[3].astype(jnp.bfloat16)
    d_act, d_steps = side_by_side((d_act_seq, d_steps_seq), TM, 0, 1, 2)
    rate_part = gradients[4]
    gain_part = gradients[5]
    d_before = d_act.astype(jnp.float32).reshape(
        frame_count, row_count, col_count, -1
    ) * silu_slope(before)
    spread_out = conv_spread(d_before, conv_kernel)
    inner_part = spread_out[:, 1 : row_count + 1, 1 : col_count + 1]
    from_below = from_behind(
        spread_out[:, :1, 1 : col_count + 1].astype(jnp.bfloat16), SPACE, -1
    ).astype(jnp.float32)
    from_above = from_behind(
        spread_out[:, row_count + 1 :, 1 : col_count + 1].astype(jnp.bfloat16), SPACE, 1
    ).astype(jnp.float32)
    d_mixed = (
        inner_part
        + jnp.pad(from_above, ((0, 0), (0, row_count - 1), (0, 0), (0, 0)))
        + jnp.pad(from_below, ((0, 0), (row_count - 1, 0), (0, 0), (0, 0)))
    )
    kernel_part = kernel_grad(d_before, padded, row_count, col_count)
    conv_bias_part = jnp.sum(d_before, axis=(0, 1, 2))
    d_raw = d_steps.astype(jnp.float32).reshape(-1, head_count) * jax.nn.sigmoid(step_raw)
    bias_part = jnp.sum(d_raw, axis=0)
    d_raw_half = d_raw.astype(jnp.bfloat16)
    d_projected = jnp.concatenate([d_gate, d_mixed.reshape(-1, d_mixed.shape[-1])], axis=1).astype(
        jnp.bfloat16
    )
    grad_input = (
        (
            lax.dot_general(d_projected, in_proj, contract_cols, preferred_element_type=jnp.float32)
            + lax.dot_general(
                d_raw_half, step_proj, contract_cols, preferred_element_type=jnp.float32
            )
        )
        .astype(jnp.bfloat16)
        .reshape(activations.shape)
    )
    summed = scatter_pairs(
        jnp.concatenate(
            [
                lax.dot_general(
                    flat_act, d_projected, contract_rows, preferred_element_type=jnp.float32
                ),
                lax.dot_general(
                    cot_flat, normed, contract_rows, preferred_element_type=jnp.float32
                ),
                lax.dot_general(
                    flat_act, d_raw_half, contract_rows, preferred_element_type=jnp.float32
                ),
            ],
            axis=1,
        ),
        ("tm_0", "tm_1", "space_0", "space_1"),
        "space_2",
        0,
    )
    grad_in_proj = summed[:, :proj_cols]
    grad_out_proj_t = summed[:, proj_cols : proj_cols + inner_w]
    grad_step_proj = summed[:, proj_cols + inner_w :]
    small_sums = together(
        (kernel_part, conv_bias_part, bias_part, rate_part, gain_part, norm_part), TM_SPACE
    )
    return (
        layer_out,
        grad_input,
        grad_in_proj,
        grad_step_proj,
        grad_out_proj_t,
        small_sums[0],
        small_sums[1],
        small_sums[2],
        small_sums[3],
        small_sums[4],
        small_sums[5],
    )


def solution(mesh):
    torus = Mesh(
        mesh.devices.reshape(2, 4, 2, 4, 2), ("tm_0", "tm_1", "space_0", "space_1", "space_2")
    )
    placed = (
        P(TM, SPACE, None, None),
        P(),
        P(),
        P(),
        P(),
        P(),
        P(),
        P(),
        P(),
        P(),
        P(TM, SPACE, None, None),
    )
    return jax.shard_map(
        on_device,
        mesh=torus,
        in_specs=placed,
        out_specs=(
            P(TM, SPACE, None, None),
            P(TM, SPACE, None, None),
            P(TM_SPACE, None),
            P(TM_SPACE, None),
            P(TM_SPACE, None),
            P(),
            P(),
            P(),
            P(),
            P(),
            P(),
        ),
        check_vma=False,
    )
```

profile of v0, /device:TPU:0, one launch (start us, length us, event | category | flops | bytes accessed | tf_op | source)
XLA Modules:
  0.0 931.5 jit_solution(12403626159152890101)
XLA Ops:
  7.2 3.3 convolution_convert_fusion
  21.5 7.6 all-to-all-start
  31.4 6.8 all-to-all-done
  47.3 132.6 %while.77 = (s32[]{:T(128)}, f32[2,16,64,64]{3,2,1,0:T(8,128)S(1)}, bf16[8,8,2,16,64]{4,1,3,2,0:T(8,128)(2,1)}, f32[8,8,8,2,16]{2,1,4,3,0:T(8,128)}, f32[8,1,8,2...) while((s32[]{:T(128)}, f32[2,16,64,64]{3,2,1,0:T(8,128)S(1)}, ...), condition=%wide.region_2.3_spmd.clone.clone.clone, body=%wide.region_0.2_spmd.clone.clone.sunk.clone | while | flops 27619172 | bytes 6108273 | solution.py:101
  50.5 3.2 bitcast_dynamic-update-slice_fusion.22
  56.9 2.8 convolution_add_fusion.10
  67.1 3.2 bitcast_dynamic-update-slice_fusion.22
  73.5 2.8 convolution_add_fusion.10
  83.8 3.2 bitcast_dynamic-update-slice_fusion.22
  90.1 2.8 convolution_add_fusion.10
  100.3 3.2 bitcast_dynamic-update-slice_fusion.22
  106.7 2.8 convolution_add_fusion.10
  116.8 3.2 bitcast_dynamic-update-slice_fusion.22
  123.2 2.8 convolution_add_fusion.10
  133.4 3.2 bitcast_dynamic-update-slice_fusion.22
  139.8 2.8 convolution_add_fusion.10
  150.0 3.2 bitcast_dynamic-update-slice_fusion.22
  156.4 2.8 convolution_add_fusion.10
  166.6 3.2 bitcast_dynamic-update-slice_fusion.22
  173.0 2.8 convolution_add_fusion.10
  182.1 12.5 %all_to_all.54 = bf16[64,2,1024]{2,1,0:T(2,128)(2,1)S(1)} all-to-all(bf16[64,2,1024]{2,1,0:T(2,128)(2,1)} %reshape.402), channel_id=1, replica_groups=mesh['tm_0'=2,'tm_1'=4,'space_0'=2,'space_1'=4,'space_2'=2] {'tm_0','tm_1'}, dimensions={0} | all-to-all | bytes 524288 | tf_op jit(solution)/shard_map/all_to_all | solution.py:209
  197.6 2.7 multiply_reduce_fusion.9
  202.2 3.6 all-to-all-start.2
  206.5 9.3 all-to-all-done.2
  220.1 234.2 %while.78 = (s32[]{:T(128)}, f32[16]{0:T(128)}, f32[16]{0:T(128)}, f32[2,16,64,64]{3,2,1,0:T(8,128)S(1)}, bf16[8,8,2,16,64]{4,1,3,2,0:T(8,128)(2,1)}, /*index=5*...) while((s32[]{:T(128)}, f32[16]{0:T(128)}, f32[16]{0:T(128)}, ...), condition=%wide.region_16.17_spmd.clone.clone.clone, body=%wide.region_5.16_spmd.clone.clone.sunk.clone | while | flops 54950372 | bytes 6407294 | solution.py:101
  221.1 4.2 fusion.255
  241.7 2.6 convolution_add_fusion.11
  250.3 4.2 fusion.255
  279.6 4.2 fusion.255
  308.9 4.2 fusion.255
  338.2 4.2 fusion.255
  358.8 2.6 convolution_add_fusion.11
  367.4 4.2 fusion.255
  388.1 2.6 convolution_add_fusion.11
  396.7 4.2 fusion.255
  426.0 4.2 fusion.255
  446.7 2.6 convolution_add_fusion.11
  459.6 4.1 all-to-all-start.3
  463.7 2.7 convolution_bitcast_fusion.8
  466.5 7.2 all-to-all-done.3
  483.1 4.3 collective-permute-done.3
  489.7 5.9 pad_maximum_fusion
  495.6 13.9 %copy.256 = f32[1024,3216]{1,0:T(8,128)} copy(f32[1024,3216]{0,1:T(8,128)} %pad_maximum_fusion) | data formatting | bytes 26345472 | tf_op jit(solution)/shard_map/concatenate | solution.py:285
  509.5 10.8 %copy.257 = f32[2,64,8,3216]{3,2,1,0:T(8,128)} copy(f32[2,64,8,3216]{3,2,0,1:T(8,128)} %bitcast.561) | data formatting | bytes 26345472 | tf_op jit(solution)/shard_map/transpose | solution.py:51
  520.5 28.5 %reduce-scatter.3.cloned.1.call-done = f32[64,8,3216]{2,1,0:T(8,128)} async-done(((f32[128,8,3216]{2,1,0:T(8,128)}), f32[64,8,3216]{2,1,0:T(8,128)}) %reduce-scatter.3.cloned.1.call-update) | async-done | bytes 6586384 | tf_op jit(solution)/shard_map/reduce_scatter | solution.py:52
  551.6 67.6 %psum.7 = f32[12592]{0:T(1024)S(1)} all-reduce(f32[12592]{0:T(1024)S(1)} %concatenate.27), channel_id=1, replica_groups=mesh['tm_0'=2,'tm_1'=4,'space_0'=2,'space_1'=4,'space_2'=2] {'tm_0','tm_..., use_global_device_ids=true, to_apply=%region_31.32 | all-reduce | flops 12592 | bytes 100736 | tf_op jit(solution)/shard_map/psum | solution.py:60
  621.7 3.8 fusion.143
  626.5 294.0 %reduce-scatter.5.cloned.1.call-done = f32[1,8,3216]{2,1,0:T(8,128)} async-done(((f32[64,8,3216]{2,1,0:T(8,128)}), f32[1,8,3216]{2,1,0:T(8,128)}) %reduce-scatter.5.cloned.1.call-update) | async-done | bytes 102928 | tf_op jit(solution)/shard_map/reduce_scatter | solution.py:53
  (659 shorter events, 334.5 us)
Async XLA Ops:
  7.2 190.4 %copy-start = (bf16[1024,1024]{1,0:T(8,128)(2,1)S(1)}, bf16[1024,1024]{1,0:T(8,128)(2,1)}, u32[]{:S(2)}) copy-start(bf16[1024,1024]{1,0:T(8,128)(2,1)} %param.24) | copy-start | bytes 6291460
  11.4 3.8 collective-permute-start
  12.7 5.2 collective-permute-start.1
  21.5 16.8 %all-to-all-start = ((bf16[8,16,1168]{2,0,1:T(8,128)(2,1)}), bf16[8,16,1168]{2,0,1:T(8,128)(2,1)S(1)}, u32[]{:S(2)}, u32[]{:S(2)}) async-start(bf16[8,16,1168]{2,0,1:T(8,128)(2,1)} %pad_maximum_fusion.4), calls=%async_computation | async-start | bytes 655360 | tf_op jit(solution)/shard_map/all_to_all | solution.py:32
  179.8 17.4 %copy-start.14 = (f32[8,8,2,64]{3,1,2,0:T(8,128)}, f32[8,8,2,64]{3,1,2,0:T(8,128)S(1)}, u32[]{:S(2)}) copy-start(f32[8,8,2,64]{3,1,2,0:T(8,128)S(1)} %get-tuple-element.2542) | copy-start | bytes 98308
  179.8 17.4 %copy-start.15 = (f32[8,8,2,64]{3,1,2,0:T(8,128)}, f32[8,8,2,64]{3,1,2,0:T(8,128)S(1)}, u32[]{:S(2)}) copy-start(f32[8,8,2,64]{3,1,2,0:T(8,128)S(1)} %get-tuple-element.2543) | copy-start | bytes 98308
  181.0 16.3 %copy-start.9 = (bf16[128,2176]{1,0:T(8,128)(2,1)S(1)}, bf16[128,2176]{1,0:T(8,128)(2,1)}, u32[]{:S(2)}) copy-start(bf16[128,2176]{1,0:T(8,128)(2,1)} %copy-done.8) | copy-start | bytes 1671172
  182.1 15.5 %copy-start.34 = (f32[1024]{0:T(1024)S(1)}, f32[1024]{0:T(1024)}, u32[]{:S(2)}) copy-start(f32[1024]{0:T(1024)} %param.23) | copy-start | bytes 12292
  202.2 13.5 %all-to-all-start.2 = ((bf16[8,16,1024]{2,0,1:T(8,128)(2,1)}), bf16[8,16,1024]{2,0,1:T(8,128)(2,1)S(1)}, u32[]{:S(2)}, u32[]{:S(2)}) async-start(bf16[8,16,1024]{2,0,1:T(8,128)(2,1)} %copy.237), calls=%async_computation.2 | async-start | bytes 524288 | tf_op jit(solution)/shard_map/all_to_all | solution.py:234
  235.3 9.1 copy-start.36
  235.3 9.1 copy-start.38
  235.3 9.1 copy-start.42
  235.3 9.1 copy-start.45
  264.5 9.1 copy-start.36
  264.5 9.1 copy-start.38
  264.5 9.1 copy-start.42
  264.5 9.1 copy-start.45
  293.8 9.1 copy-start.36
  293.8 9.1 copy-start.38
  293.8 9.1 copy-start.42
  293.8 9.2 copy-start.45
  323.1 9.1 copy-start.36
  323.1 9.1 copy-start.38
  323.1 9.1 copy-start.42
  323.1 9.1 copy-start.45
  352.4 9.1 copy-start.45
  381.6 9.1 copy-start.36
  381.6 9.1 copy-start.38
  381.6 9.1 copy-start.42
  381.6 9.1 copy-start.45
  410.9 9.1 copy-start.36
  410.9 9.1 copy-start.38
  410.9 9.2 copy-start.42
  410.9 9.2 copy-start.45
  440.2 9.1 copy-start.36
  440.2 9.1 copy-start.38
  440.2 9.1 copy-start.42
  440.2 9.1 copy-start.45
  454.3 9.3 %copy-start.5 = (f32[128,1024]{1,0:T(8,128)S(1)}, f32[128,1024]{1,0:T(8,128)}, u32[]{:S(2)}) copy-start(f32[128,1024]{1,0:T(8,128)} %copy-done.4) | copy-start | bytes 1572868
  454.3 9.4 %copy-start.13 = (bf16[8,2,8,1024]{3,2,1,0:T(8,128)(2,1)S(1)}, bf16[8,2,8,1024]{3,2,1,0:T(8,128)(2,1)}, u32[]{:S(2)}) copy-start(bf16[8,2,8,1024]{3,2,1,0:T(8,128)(2,1)} %param.25) | copy-start | bytes 786436
  454.4 9.4 %copy-start.35 = (f32[1024]{0:T(1024)S(1)}, f32[1024]{0:T(1024)}, u32[]{:S(2)}) copy-start(f32[1024]{0:T(1024)} %param.23) | copy-start | bytes 12292
  454.4 9.3 %copy-start.52 = (f32[128]{0:T(128)S(1)}, f32[128]{0:T(128)}, u32[]{:S(2)}) copy-start(f32[128]{0:T(128)} %copy-done.51) | copy-start | bytes 1540
  459.6 14.1 %all-to-all-start.3 = ((bf16[64,2,1168]{2,1,0:T(2,128)(2,1)}), bf16[64,2,1168]{2,1,0:T(2,128)(2,1)}, u32[]{:S(2)}, u32[]{:S(2)}) async-start(bf16[64,2,1168]{2,1,0:T(2,128)(2,1)} %copy.251), calls=%async_computation.3 | async-start | bytes 655360 | tf_op jit(solution)/shard_map/all_to_all | solution.py:32
  463.6 85.4 %reduce-scatter.3.cloned.1.call-start = ((), (), s32[]{:S(2)}) async-start(), calls=%async_computation.6 | async-start | bytes 20447232 | tf_op jit(solution)/shard_map/reduce_scatter | solution.py:52
  466.5 9.3 %copy-start.2 = (f32[8,4,8,1152]{3,2,1,0:T(8,128)S(1)}, f32[8,4,8,1152]{3,2,1,0:T(8,128)}, u32[]{:S(2)}) copy-start(f32[8,4,8,1152]{3,2,1,0:T(8,128)} %copy-done.1) | copy-start | bytes 3538948
  479.6 3.5 collective-permute-start.2
  481.3 6.1 collective-permute-start.3
  520.4 400.1 %reduce-scatter.5.cloned.1.call-start = ((), (), s32[]{:S(2)}) async-start(), calls=%async_computation.7 | async-start | bytes 6922240 | tf_op jit(solution)/shard_map/reduce_scatter | solution.py:53
  (58 other events, 266.7 us)
Sparse Core Ops, SparseCore 0:
  520.5 28.4 reduce-scatter.2
  551.4 369.0 reduce-scatter.4
where the time goes:
time: 939 us; the launch traced here: 931 us
  waiting for transfers between devices  353 us (38%)
  matrix products  223 us (24%)
  other arithmetic  124 us (13%)
  local copies, waits for them, and re-layouts  115 us (12%)
  blocking collectives  80.1 us (9%)
  starting transfers between devices  21.1 us (2%)
  between operations  15.1 us (2%)
    reduce_scatter x1, waiting for transfers between devices, scatter_pairs(): return lax.psum_scatter(parts, chips, scatter_dimension=0, tiled=True)[0]  294 us
    dot_general x24, matrix products, ssd_block(): jnp.einsum('skh,skhp,skn->khpn', tail_weight, heads_in, b_proj, precision...  68.4 us
    psum x1, blocking collectives, together(): total = lax.psum(jnp.concatenate([a.ravel() for a in arrays]), axis)  67.6 us
    dot_general x24, matrix products, ssd_block(): jnp.einsum('tkn,khpn->tkhp', c_proj, state_in, precision=top_precision)  62.6 us
    dynamic_update_slice x56, other arithmetic, ssd_sequence(): lax.scan(advance, start_state, (fold_blocks(heads_in), fold_blocks(b_proj...  59.6 us
    dot_general x24, matrix products, ssd_block(): jnp.einsum('tskh,skhp->tkhp', weights * inner_cb[..., None], heads_in, pr...  49.9 us
    reduce_scatter x1, waiting for transfers between devices, scatter_pairs(): parts = lax.psum_scatter(parts, core, scatter_dimension=0, tiled=True)  28.5 us
    dot_general x24, matrix products, ssd_block(): jnp.einsum('tkn,skn->tsk', c_proj, b_proj, precision=top_precision)  24.7 us
  transfers between devices with their start and end apart: 9, of which 7 were waited for; matrix products, arithmetic and copies ran while one was open for 2% of the time, Pallas kernels for 0%

commit v1 on v0

v1 whole, which is shorter than its diff:
```python
import jax
import jax.numpy as jnp
from jax import lax
from jax.experimental import pallas as pl
from jax.experimental.pallas import tpu as pltpu
from jax.sharding import Mesh
from jax.sharding import PartitionSpec as P

SPACE = ("space_0", "space_1", "space_2")
TM = ("tm_0", "tm_1")
TM_SPACE = ("tm_0", "tm_1", "space_0", "space_1", "space_2")
CHIPS = ("tm_0", "tm_1", "space_0", "space_1")
CORE = "space_2"

HIGH = lax.Precision.HIGHEST
NORM_EPS = 1e-05
F32 = jnp.float32
BF16 = jnp.bfloat16
VMEM = pl.BlockSpec(memory_space=pltpu.VMEM)
SMEM = pl.BlockSpec(memory_space=pltpu.SMEM)
LANES = 128


def shape_of(dims, dtype):
    return jax.ShapeDtypeStruct(dims, dtype)


def iota(dims, axis):
    return lax.broadcasted_iota(jnp.int32, dims, axis)


def call(body, out_shape, *args, flops=1 << 20, smem=()):
    specs = [SMEM if k in smem else VMEM for k in range(len(args))]
    outs = jax.tree.map(lambda _: VMEM, out_shape)
    moved = sum(a.size * a.dtype.itemsize for a in args)
    moved += sum(o.size * o.dtype.itemsize for o in jax.tree.leaves(out_shape))
    return pl.pallas_call(
        body,
        out_shape=out_shape,
        in_specs=specs,
        out_specs=outs,
        cost_estimate=pl.CostEstimate(flops=flops, bytes_accessed=moved, transcendentals=0),
    )(*args)


def dot_nt(a, b, precision=None):
    return lax.dot_general(
        a, b, (((1,), (1,)), ((), ())), precision=precision, preferred_element_type=F32
    )


def dot_tn(a, b, precision=None):
    return lax.dot_general(
        a, b, (((0,), (0,)), ((), ())), precision=precision, preferred_element_type=F32
    )


def dot_nn(a, b, precision=None):
    return jnp.dot(a, b, precision=precision, preferred_element_type=F32)


def sigmoid(x):
    return 1.0 / (1.0 + jnp.exp(-x))


def conv_body(low_ref, mid_ref, high_ref, kernel_ref, bias_ref, act_ref, slope_ref):
    rows, cols = mid_ref.shape[:2]
    channels = mid_ref.shape[3]

    def chunk(k, carry):
        lanes = pl.ds(pl.multiple_of(k * LANES, LANES), LANES)
        taps = [kernel_ref[t : t + 1, lanes] for t in range(9)]
        bias = bias_ref[0:1, lanes]
        grid = [
            [low_ref[c, :, lanes].astype(F32) for c in range(cols)],
            *[[mid_ref[r, c, :, lanes].astype(F32) for c in range(cols)] for r in range(rows)],
            [high_ref[c, :, lanes].astype(F32) for c in range(cols)],
        ]
        for r in range(rows):
            for c in range(cols):
                total = None
                for i in range(3):
                    for j in range(3):
                        if 0 <= c + j - 1 < cols:
                            term = taps[3 * i + j] * grid[r + i][c + j - 1]
                            total = term if total is None else total + term
                before = total + bias
                gate = sigmoid(before)
                act_ref[r, c, :, lanes] = (before * gate).astype(BF16)
                slope_ref[r, c, :, lanes] = gate * (1.0 + before * (1.0 - gate))
        return carry

    lax.fori_loop(0, channels // LANES, chunk, 0)


def conv_grad_body(moved_ref, slope_ref, low_ref, mid_ref, high_ref, before_ref, sums_ref):
    rows, cols = mid_ref.shape[:2]
    channels = mid_ref.shape[3]

    def chunk(k, carry):
        lanes = pl.ds(pl.multiple_of(k * LANES, LANES), LANES)
        grid = [
            [low_ref[c, :, lanes].astype(F32) for c in range(cols)],
            *[[mid_ref[r, c, :, lanes].astype(F32) for c in range(cols)] for r in range(rows)],
            [high_ref[c, :, lanes].astype(F32) for c in range(cols)],
        ]
        sums = [None] * 10
        for r in range(rows):
            for c in range(cols):
                d_before = moved_ref[r, c, :, lanes].astype(F32) * slope_ref[r, c, :, lanes]
                before_ref[r, c, :, lanes] = d_before.astype(BF16)
                for i in range(3):
                    for j in range(3):
                        if 0 <= c + j - 1 < cols:
                            term = d_before * grid[r + i][c + j - 1]
                            t = 3 * i + j
                            sums[t] = term if sums[t] is None else sums[t] + term
                sums[9] = d_before if sums[9] is None else sums[9] + d_before
        for t in range(10):
            sums_ref[t : t + 1, lanes] = jnp.sum(sums[t], axis=0, keepdims=True)
        return carry

    lax.fori_loop(0, channels // LANES, chunk, 0)


def conv_spread_body(low_ref, high_ref, moved_ref, slope_ref, kernel_ref, out_ref):
    rows, cols = moved_ref.shape[:2]
    channels = slope_ref.shape[3]

    def chunk(k, carry):
        lanes = pl.ds(pl.multiple_of(k * LANES, LANES), LANES)
        taps = [kernel_ref[t : t + 1, lanes] for t in range(9)]
        grid = [
            [low_ref[c, :, lanes].astype(F32) for c in range(cols)],
            *[
                [
                    moved_ref[r, c, :, lanes].astype(F32) * slope_ref[r, c, :, lanes]
                    for c in range(cols)
                ]
                for r in range(rows)
            ],
            [high_ref[c, :, lanes].astype(F32) for c in range(cols)],
        ]
        for r in range(rows):
            for c in range(cols):
                total = None
                for i in range(3):
                    for j in range(3):
                        if 0 <= c + 1 - j < cols:
                            term = taps[3 * i + j] * grid[r + 2 - i][c + 1 - j]
                            total = term if total is None else total + term
                out_ref[r, c, :, lanes] = total.astype(BF16)
        return carry

    lax.fori_loop(0, channels // LANES, chunk, 0)
    tail = slice(channels, out_ref.shape[3])
    for r in range(rows):
        for c in range(cols):
            out_ref[r, c, :, tail] = moved_ref[r, c, :, tail]


def head_select(heads, width):
    dims = (heads, heads * width)
    return (iota(dims, 1) // width == iota(dims, 0)).astype(F32)


def decay_body(step_ref, rate_ref, decay_ref, weight_ref):
    tokens = step_ref.shape[1]
    frames = step_ref.shape[0] * step_ref.shape[2]
    heads = step_ref.shape[3]
    pairs = heads // 2
    wide = 2 * frames
    place = iota((frames, frames), 0)
    other = iota((frames, frames), 1)
    lower = (place >= other).astype(F32)
    row2 = iota((frames, wide), 0)
    lane2 = iota((frames, wide), 1)
    inner2 = jnp.where(lane2 < frames, lane2, lane2 - frames)
    upper2 = (row2 <= inner2).astype(F32)
    eye2 = (row2 == inner2).astype(F32)
    causal = row2 >= inner2
    first = lax.broadcasted_iota(jnp.int32, (1, wide), 1) < frames
    select = head_select(heads, frames)
    for tok in range(tokens):
        steps = step_ref[:, tok].reshape(frames, heads)
        decay = steps * rate_ref[...]
        running = dot_nn(lower, decay, HIGH)
        running_t = dot_tn(decay, upper2, HIGH)
        steps_t = dot_tn(steps, eye2, HIGH)
        spread_cols = dot_nn(running, select, HIGH)
        for j in range(pairs):
            row = jnp.where(first, running_t[2 * j : 2 * j + 1], running_t[2 * j + 1 : 2 * j + 2])
            step_row = jnp.where(first, steps_t[2 * j : 2 * j + 1], steps_t[2 * j + 1 : 2 * j + 2])
            spread = spread_cols[:, j * wide : (j + 1) * wide] - row
            kept = jnp.where(causal, jnp.exp(-jnp.where(causal, spread, 0.0)), 0.0)
            decay_ref[tok, j] = kept
            weight_ref[tok, j] = kept * step_row


def unpack(tok_values, frames, inner):
    lane = iota((frames, LANES), 1)
    left = lane < LANES // 2
    mixed = tok_values[:, inner : inner + LANES]
    swapped = pltpu.roll(mixed, LANES // 2, 1)
    b_left = jnp.where(left, mixed, 0.0)
    c_left = jnp.where(left, swapped, 0.0)
    b_right = jnp.where(left, 0.0, swapped)
    return left, b_left, c_left, b_right


def score(b_left, c_left):
    both = jnp.concatenate([b_left, b_left], axis=0).astype(BF16)
    return dot_nt(c_left.astype(BF16), both)


def block_diag(pair, left):
    zero = jnp.zeros_like(pair)
    return jnp.concatenate([jnp.where(left, pair, zero), jnp.where(left, zero, pair)], axis=0)


def forward_body(
    act_ref, weight_ref, gate_ref, cot_ref, skip_ref, gain_ref, factor_ref, d_ssd_ref, intra_ref, part_ref
):
    tokens = act_ref.shape[1]
    frames = act_ref.shape[0] * act_ref.shape[2]
    inner = gate_ref.shape[3]
    pairs = weight_ref.shape[1]
    part = None
    for tok in range(tokens):
        values = act_ref[:, tok].astype(F32).reshape(frames, inner + LANES)
        left, b_left, c_left, _ = unpack(values, frames, inner)
        scores = score(b_left, c_left)
        for j in range(pairs):
            lanes = slice(j * LANES, (j + 1) * LANES)
            pair = values[:, lanes]
            mix = (weight_ref[tok, j] * scores).astype(BF16)
            intra_ref[tok, :, lanes] = dot_nn(mix, block_diag(pair, left).astype(BF16))
        ssd = (intra_ref[tok] + skip_ref[...] * values[:, :inner]).astype(BF16).astype(F32)
        gate = gate_ref[:, tok].astype(F32).reshape(frames, inner)
        squashed = sigmoid(gate)
        opened = gate * squashed
        gated = ssd * opened
        scale = lax.rsqrt(jnp.mean(gated * gated, axis=-1, keepdims=True) + NORM_EPS)
        unit = gated * scale
        gain = gain_ref[...]
        cot = cot_ref[:, tok].reshape(frames, inner)
        term = jnp.sum(cot * unit, axis=0, keepdims=True)
        part = term if part is None else part + term
        pulled = cot * gain
        along = jnp.mean(pulled * unit, axis=-1, keepdims=True)
        d_gated = scale * (pulled - unit * along)
        d_ssd_ref[tok] = (d_gated * opened).astype(BF16)
        d_gate = d_gated * ssd * (squashed * (1.0 + gate * (1.0 - squashed)))
        blocks = (act_ref.shape[0], act_ref.shape[2], inner)
        factor_ref[:, tok, :, :inner] = (unit * gain).reshape(blocks).astype(BF16)
        factor_ref[:, tok, :, inner:] = d_gate.reshape(blocks).astype(BF16)
    part_ref[...] = part


def backward_body(
    act_ref,
    decay_ref,
    weight_ref,
    intra_ref,
    d_ssd_ref,
    step_ref,
    raw_ref,
    rate_ref,
    skip_ref,
    out_ref,
    small_ref,
    pulled_ref,
):
    tokens = act_ref.shape[1]
    blocks, per = act_ref.shape[0], act_ref.shape[2]
    frames = blocks * per
    heads = step_ref.shape[3]
    inner = intra_ref.shape[2]
    pairs = heads // 2
    width = inner // heads
    select = head_select(heads, width)
    dims = (frames, frames)
    upper = (iota(dims, 0) <= iota(dims, 1)).astype(F32)
    small = [None, None, None]

    def add(k, term):
        small[k] = term if small[k] is None else small[k] + term

    for tok in range(tokens):
        values = act_ref[:, tok].astype(F32).reshape(frames, inner + LANES)
        left, b_left, c_left, b_right = unpack(values, frames, inner)
        scores = score(b_left, c_left)
        d_scores = jnp.zeros((frames, LANES), F32)
        for j in range(pairs):
            lanes = slice(j * LANES, (j + 1) * LANES)
            pair = values[:, lanes]
            d_pair = d_ssd_ref[tok, :, lanes]
            diag = block_diag(pair, left).astype(BF16)
            d_scores = d_scores + dot_nt(d_pair, diag) * weight_ref[tok, j]
            mix = (decay_ref[tok, j] * scores).astype(BF16)
            wide = dot_tn(mix, d_pair)
            pulled_ref[:, lanes] = jnp.where(left, wide[:frames], wide[frames:])
        u = values[:, :inner]
        dy = d_ssd_ref[tok].astype(F32)
        pulled = pulled_ref[...]
        steps = step_ref[:, tok].reshape(frames, heads)
        rate = rate_ref[...]
        du = dot_nn(steps, select, HIGH) * pulled + skip_ref[...] * dy
        out_ref[:, tok, :, :inner] = du.reshape(blocks, per, inner).astype(BF16)
        q = dot_nt(dy * intra_ref[tok], select, HIGH)
        r = dot_nt(u * pulled, select, HIGH)
        add(2, dot_nt(jnp.sum(dy * u, axis=0, keepdims=True), select, HIGH))
        d_decay = dot_nn(upper, steps * r - q, HIGH)
        add(1, jnp.sum(d_decay * steps, axis=0, keepdims=True))
        d_steps = (r + rate * d_decay).astype(BF16).astype(F32)
        d_raw = d_steps * sigmoid(raw_ref[:, tok].reshape(frames, heads))
        add(0, jnp.sum(d_raw, axis=0, keepdims=True))
        folded = d_scores + pltpu.roll(d_scores, LANES // 2, 1)
        folded = jnp.where(left, folded, 0.0).astype(BF16)
        stacked = jnp.concatenate([b_right, jnp.zeros_like(b_right)], axis=0).astype(BF16)
        d_bc = dot_nn(folded, stacked) + dot_tn(folded, c_left.astype(BF16))[:frames]
        out_ref[:, tok, :, inner : inner + LANES] = d_bc.reshape(blocks, per, LANES).astype(BF16)
        padded = jnp.concatenate([d_raw, jnp.zeros((frames, LANES - heads), F32)], axis=1)
        out_ref[:, tok, :, inner + LANES :] = padded.reshape(blocks, per, LANES).astype(BF16)
    for k in range(3):
        small_ref[k : k + 1, :] = small[k]


def outer_body(core_ref, left_ref, left2_ref, right_ref, right2_ref, out_ref, *, swap):
    rows = left_ref.shape[1]
    cols = right_ref.shape[1]
    groups = out_ref.shape[0]
    core = core_ref[0, 0]
    left_half = rows // swap
    col_half = cols // swap
    step = LANES
    for part in range(swap):
        right = right_ref[:, part * col_half : (part + 1) * col_half]
        right2 = right2_ref[:, part * col_half : (part + 1) * col_half]
        base = (swap - 1 - part) * left_half

        def block(k, carry):
            lanes = pl.ds(pl.multiple_of(base + k * step, step), step)
            total = dot_tn(left_ref[:, lanes], right) + dot_tn(left2_ref[:, lanes], right2)
            split = total.reshape(step // 16, 2, 8, col_half)
            chosen = jnp.where(core == 0, split[:, 0], split[:, 1]).astype(BF16)
            out_ref[pl.ds(k * (step // 16), step // 16), :, part * col_half : (part + 1) * col_half] = chosen
            return carry

        lax.fori_loop(0, groups * 16 // step, block, 0)


def outer(core, left, left2, right, right2, swap):
    groups = left.shape[1] // swap // 16

    def body(*refs):
        outer_body(*refs, swap=swap)

    flops = 4 * left.shape[0] * left.shape[1] // swap * right.shape[1]
    return call(
        body, shape_of((groups, 8, right.shape[1]), BF16), core, left, left2, right, right2, flops=flops, smem=(0,)
    )


def exchange(array, axis):
    return lax.all_to_all(array, axis, split_axis=0, concat_axis=0, tiled=True)


def on_device(
    activations,
    in_proj,
    step_proj,
    step_bias,
    decay_rates,
    conv_kernel,
    conv_bias,
    skip_gain,
    norm_gain,
    out_proj,
    out_cotangent,
):
    frame_count, row_count, col_count, model_width = activations.shape
    inner = out_proj.shape[0]
    heads = step_proj.shape[1]
    channels = conv_bias.shape[0]
    tokens = row_count * col_count
    tm_size = lax.axis_size(TM)
    own = tokens // tm_size
    frames = frame_count * tm_size
    wide = channels + LANES
    grid4 = (row_count, col_count, frame_count)
    tok4 = (tm_size, own, frame_count)
    flat = tokens * frame_count
    core = lax.axis_index(CORE).astype(jnp.int32).reshape(1, 1)
    swap_core = [(0, 1), (1, 0)]
    devices = lax.axis_size(SPACE)
    upward = [(i, i + 1) for i in range(devices - 1)]
    downward = [(b, a) for a, b in upward]

    act = activations.transpose(1, 2, 0, 3).reshape(tokens, frame_count, model_width)
    cot = out_cotangent.transpose(1, 2, 0, 3).reshape(tokens, frame_count, model_width)
    gate_proj, mix_proj = in_proj[:, :inner], in_proj[:, inner:]
    kernel9 = conv_kernel.reshape(9, channels)
    bias1 = conv_bias.reshape(1, channels)

    act_flat = act.reshape(flat, model_width)
    mixed = dot_nn(act_flat, mix_proj).astype(BF16).reshape(*grid4, channels)
    low = lax.ppermute(mixed[row_count - 1], SPACE, upward)
    high = lax.ppermute(mixed[0], SPACE, downward)
    activated, slope = call(
        conv_body,
        (shape_of((*grid4, channels), BF16), shape_of((*grid4, channels), F32)),
        low,
        mixed,
        high,
        kernel9,
        bias1,
    )

    source = exchange(jnp.concatenate([act, cot], axis=-1), TM).reshape(flat, 2 * model_width)
    act_tok, cot_tok = source[:, :model_width], source[:, model_width:]
    gate = dot_nn(act_tok, gate_proj).astype(BF16)
    raw = dot_nn(act_tok, step_proj) + step_bias
    steps = jax.nn.softplus(raw).astype(BF16).astype(F32)
    d_normed = dot_nt(cot_tok, out_proj)
    rate1 = decay_rates.reshape(1, heads)
    skip1 = jnp.repeat(skip_gain, inner // heads).reshape(1, inner)
    gain1 = norm_gain.reshape(1, inner)
    steps4 = steps.reshape(*tok4, heads)
    square = shape_of((own, heads // 2, frames, 2 * frames), F32)
    decay, weight = call(decay_body, (square, square), steps4, rate1)

    moved = exchange(activated.reshape(tokens, frame_count, channels), TM)
    moved = moved.reshape(*tok4, channels)
    factor, d_ssd, intra, norm_part = call(
        forward_body,
        (
            shape_of((*tok4, 2 * inner), BF16),
            shape_of((own, frames, inner), BF16),
            shape_of((own, frames, inner), F32),
            shape_of((1, inner), F32),
        ),
        moved,
        weight,
        gate.reshape(*tok4, inner),
        d_normed.reshape(*tok4, inner),
        skip1,
        gain1,
        flops=1 << 26,
    )
    back = pl.pallas_call(
        backward_body,
        out_shape=(shape_of((*tok4, wide), BF16), shape_of((3, heads), F32)),
        in_specs=[VMEM] * 9,
        out_specs=(VMEM, VMEM),
        scratch_shapes=[pltpu.VMEM((frames, inner), F32)],
        cost_estimate=pl.CostEstimate(flops=1 << 27, bytes_accessed=1 << 22, transcendentals=0),
    )(moved, decay, weight, intra, d_ssd, steps4, raw.reshape(*tok4, heads), rate1, skip1)
    d_moved, small_part = back
    returned = exchange(d_moved.reshape(tokens, frame_count, wide), TM).reshape(*grid4, wide)

    factor_flat = factor.reshape(flat, 2 * inner)
    normed = factor_flat[:, :inner]
    d_gate_tok = factor_flat[:, inner:]
    layer_tok = dot_nn(normed, out_proj).astype(BF16)
    home = exchange(
        jnp.concatenate([layer_tok, d_gate_tok], axis=1).reshape(tokens, frame_count, 2 * inner), TM
    )
    layer_out = home[..., :inner].reshape(*grid4, inner).transpose(2, 0, 1, 3)
    d_gate = home[..., inner:].reshape(flat, inner)
    source2 = lax.ppermute(source, CORE, swap_core)
    factor2 = lax.ppermute(factor_flat, CORE, swap_core)
    early = exchange(outer(core, source, source2, factor_flat, factor2, 2), CHIPS)
    early_sum = jnp.sum(early.astype(F32), axis=0)

    d_before, conv_part = call(
        conv_grad_body,
        (shape_of((*grid4, channels), BF16), shape_of((10, channels), F32)),
        returned,
        slope,
        low,
        mixed,
        high,
    )
    d_low = lax.ppermute(d_before[row_count - 1], SPACE, upward)
    d_high = lax.ppermute(d_before[0], SPACE, downward)
    late_factor = call(
        conv_spread_body,
        shape_of((*grid4, wide), BF16),
        d_low,
        d_high,
        returned,
        slope,
        kernel9,
    ).reshape(flat, wide)
    act2 = lax.ppermute(act_flat, CORE, swap_core)
    late2 = lax.ppermute(late_factor, CORE, swap_core)
    late = exchange(outer(core, act_flat, act2, late_factor, late2, 1), CHIPS)
    late_sum = jnp.sum(late.astype(F32), axis=0)

    back_proj = jnp.concatenate(
        [mix_proj, step_proj, jnp.zeros((model_width, LANES - heads), BF16)], axis=1
    )
    grad_input = (dot_nt(late_factor, back_proj) + dot_nt(d_gate, gate_proj)).astype(BF16)
    grad_input = grad_input.reshape(*grid4, model_width).transpose(2, 0, 1, 3)

    grad_in_proj = jnp.concatenate([early_sum[:, inner:], late_sum[:, :channels]], axis=1)
    grad_step_proj = late_sum[:, channels : channels + heads]
    grad_out_proj_t = early_sum[:, :inner]

    pieces = [conv_part.ravel(), norm_part.ravel(), small_part.ravel()]
    count = lax.axis_size(TM_SPACE)
    size = sum(p.size for p in pieces)
    each = -(-size // (count * LANES)) * LANES
    pieces.append(jnp.zeros((count * each - size,), F32))
    shares = exchange(jnp.concatenate(pieces).reshape(count, 1, each), TM_SPACE)
    share = jnp.sum(shares, axis=0, keepdims=True)
    totals = exchange(jnp.broadcast_to(share, (count, 1, each)), TM_SPACE).ravel()
    at = 9 * channels
    grad_conv_kernel = totals[:at].reshape(3, 3, channels)
    grad_conv_bias = totals[at : at + channels]
    at += channels
    grad_norm_gain = totals[at : at + inner]
    at += inner
    grad_step_bias = totals[at : at + heads]
    grad_decay = totals[at + heads : at + 2 * heads]
    grad_skip = totals[at + 2 * heads : at + 3 * heads]
    return (
        layer_out,
        grad_input,
        grad_in_proj,
        grad_step_proj,
        grad_out_proj_t,
        grad_conv_kernel,
        grad_conv_bias,
        grad_step_bias,
        grad_decay,
        grad_skip,
        grad_norm_gain,
    )


def solution(mesh):
    torus = Mesh(
        mesh.devices.reshape(2, 4, 2, 4, 2), ("tm_0", "tm_1", "space_0", "space_1", "space_2")
    )
    split = P(TM, SPACE, None, None)
    placed = (split, P(), P(), P(), P(), P(), P(), P(), P(), P(), split)
    rows = P(TM_SPACE, None)
    return jax.shard_map(
        on_device,
        mesh=torus,
        in_specs=placed,
        out_specs=(split, split, rows, rows, rows, P(), P(), P(), P(), P(), P()),
        check_vma=False,
    )
```

time: 939 us -> 195 us (0.21)
  waiting for transfers between devices: 353 us -> 47.3 us
  matrix products: 223 us -> 10.7 us
  other arithmetic: 124 us -> 4.48 us
  local copies, waits for them, and re-layouts: 115 us -> 32.7 us
  blocking collectives: 80.1 us -> 0 us
  starting transfers between devices: 21.1 us -> 64.9 us
  Pallas kernels: 0 us -> 32.3 us
  between operations: 15.1 us -> 0.98 us
    reduce_scatter x2 -> x0, waiting for transfers between devices: 323 us -> none  [the longest x1 294 us: scatter_pairs(): return lax.psum_scatter(parts, chips, scatter_dimension=0, tiled=True)[0]]
    dot_general x105 -> x7, matrix products: 223 us -> 10.7 us  [the longest x4 5.57 us: dot_nn(): return jnp.dot(a, b, precision=precision, preferred_element_type=F32)]
    psum x1 -> x0, blocking collectives: 67.6 us -> none  [together(): total = lax.psum(jnp.concatenate([a.ravel() for a in arrays]), axis)]
    dynamic_update_slice x56 -> x0, other arithmetic: 59.6 us -> none  [ssd_sequence(): lax.scan(advance, start_state, (fold_blocks(heads_in), fold_blocks(b_proj...]
    all_to_all x3 -> x8, starting transfers between devices: 15.3 us -> 54.4 us  [exchange(): return lax.all_to_all(array, axis, split_axis=0, concat_axis=0, tiled=True)]
    pallas_call x0 -> x8, Pallas kernels: none -> 32.3 us  [the longest x7 27.5 us: call(): pl.pallas_call(body, out_shape=out_shape, in_specs=specs, out_specs=outs,...]
    reduce_sum x19 -> x3, other arithmetic: 24.9 us -> 2.14 us  [the longest x1 1.9 us: on_device(): early_sum = jnp.sum(early.astype(F32), axis=0)]
    dynamic_slice x48 -> x0, local copies, waits for them, and re-layouts: 20.5 us -> none  [ssd_sequence(): lax.scan(advance, start_state, (fold_blocks(heads_in), fold_blocks(b_proj...]
  transfers between devices with their start and end apart: 9 -> 16, of which waited for: 7 -> 10; matrix products, arithmetic and copies ran while one was open for 2% -> 18% of each run, Pallas kernels for 0% -> 11%
where the time goes in v1:
time: 195 us; the launch traced here: 193 us
  starting transfers between devices  64.9 us (33%)
  waiting for transfers between devices  47.3 us (24%)
  local copies, waits for them, and re-layouts  32.7 us (17%)
  Pallas kernels  32.3 us (17%)
  matrix products  10.7 us (5%)
  other arithmetic  4.48 us (2%)
    all_to_all x8, starting transfers between devices, exchange(): return lax.all_to_all(array, axis, split_axis=0, concat_axis=0, tiled=True)  54.4 us
    all_to_all x8, waiting for transfers between devices, exchange(): return lax.all_to_all(array, axis, split_axis=0, concat_axis=0, tiled=True)  43.1 us
    pallas_call x7, Pallas kernels, call(): pl.pallas_call(body, out_shape=out_shape, in_specs=specs, out_specs=outs,...  27.5 us
    dot_general x4, matrix products, dot_nn(): return jnp.dot(a, b, precision=precision, preferred_element_type=F32)  5.57 us
    unnamed x45, local copies, waits for them, and re-layouts  5.35 us
    concatenate x1, local copies, waits for them, and re-layouts, on_device(): jnp.concatenate([mix_proj, step_proj, jnp.zeros((model_width, LANES - hea...  5.13 us
    dot_general x3, matrix products, dot_nt(): lax.dot_general(a, b, (((1,), (1,)), ((), ())), precision=precision, pref...  5.09 us
    pallas_call x1, Pallas kernels, on_device(): pl.pallas_call(backward_body, out_shape=(shape_of((*tok4, wide), BF16), s...  4.81 us
  transfers between devices with their start and end apart: 16, of which 10 were waited for; matrix products, arithmetic and copies ran while one was open for 18% of the time, Pallas kernels for 11%

profile of v1, /device:TPU:0, one launch (start us, length us, event | category | flops | bytes accessed | tf_op | source)
XLA Modules:
  0.0 193.3 jit_solution(6184156110988315170)
XLA Ops:
  0.7 1.3 copy.56
  1.9 1.1 copy.55
  3.0 0.9 pad_maximum_fusion
  3.9 7.7 %all-to-all-start.1 = ((bf16[16,8,2048]{2,1,0:T(8,128)(2,1)}), bf16[16,8,2048]{2,1,0:T(8,128)(2,1)S(1)}, u32[]{:S(2)}, u32[]{:S(2)}) async-start(bf16[16,8,2048]{2,1,0:T(8,128)(2,1)} %pad_maximum_fusion), calls=%async_computation.1 | async-start | bytes 1048576 | tf_op jit(solution)/shard_map/all_to_all | solution.py:366
  12.5 2.2 %convolution_convert_fusion = bf16[128,1152]{1,0:T(8,128)(2,1)S(1)} fusion(bf16[128,1024]{1,0:T(8,128)(2,1)S(1)} %bitcast.78, bf16[1024,2176]{1,0:T(8,128)(2,1)} %param.12), kind=kOutput, calls=%fused_computation.2 | convolution fusion | flops 302137344 | bytes 2916352 | tf_op jit(solution)/shard_map/dot_general | solution.py:59
  14.7 1.3 collective-permute-start.1
  16.0 3.0 %collective-permute-start = (bf16[8,8,1152]{2,1,0:T(8,128)(2,1)S(1)}, bf16[8,8,1152]{2,1,0:T(8,128)(2,1)S(1)}, u32[]{:S(2)}, u32[]{:S(2)}) collective-permute-start(bf16[8,8,1152]{2,1,0:T(8,128)(2,1)S(1)} %get-tuple-element.38), channel_id=1, source_target_pairs={{0,1},{1,2},{2,3},{3,4},{4,5},{5,6},{6,7},{7,8},{8,9},{9,10},{10,1... | collective-permute-start | bytes 442376 | tf_op jit(solution)/shard_map/ppermute | solution.py:408
  20.4 1.5 reshape.126.kernel_ref
  22.6 2.7 %shard_map.194 = (bf16[2,8,8,1152]{3,2,1,0:T(8,128)(2,1)}, f32[2,8,8,1152]{3,2,1,0:T(8,128)}) custom-call(bf16[8,8,1152]{2,1,0:T(8,128)(2,1)} %copy-done.13, bf16[2,8,8,1152]{3,2,1,0:T(8,128)(2,1)} %bitcast.68, bf16[8,8,1152]{2,1,0:T(8,128)(2,1)} %copy-done.12, f32[9,1152]{1,0:T(8,128)} %reshape.126.kernel_ref, f32[1,1152]{1,0:T(1,128)} %reshape.127.bias_ref), custom_call_target="tpu_custom_call" | custom-call | flops 1048576 | bytes 1520640 | tf_op jit(solution)/shard_map/pallas_call | solution.py:37
  25.4 7.2 %all-to-all-start = ((bf16[16,8,1152]{2,1,0:T(8,128)(2,1)}), bf16[16,8,1152]{2,1,0:T(8,128)(2,1)S(1)}, u32[]{:S(2)}, u32[]{:S(2)}) async-start(bf16[16,8,1152]{2,1,0:T(8,128)(2,1)} %bitcast.84), calls=%async_computation | async-start | bytes 589824 | tf_op jit(solution)/shard_map/all_to_all | solution.py:366
  34.3 1.6 fusion.9
  35.9 2.8 %shard_map.195 = (f32[2,8,64,128]{3,2,1,0:T(8,128)}, f32[2,8,64,128]{3,2,1,0:T(8,128)}) custom-call(f32[8,2,8,16]{3,2,1,0:T(8,128)} %bitcast.81, f32[1,16]{1,0:T(1,128)} %bitcast.96), custom_call_target="tpu_custom_call" | custom-call | flops 1048576 | bytes 1056832 | tf_op jit(solution)/shard_map/pallas_call | solution.py:37
  38.6 2.7 %fusion.5 = bf16[128,1024]{1,0:T(8,128)(2,1)} fusion(bf16[1024,2176]{1,0:T(8,128)(2,1)} %param.12, bf16[128,2048]{1,0:T(8,128)(2,1)S(1)} %bitcast.58), kind=kOutput, calls=%fused_computation.9 | convolution fusion | flops 268566528 | bytes 2621440 | tf_op jit(solution)/shard_map/dot_general | solution.py:59
  41.4 1.7 all-to-all-done
  43.8 3.4 %shard_map.196 = (bf16[8,2,8,2048]{3,2,1,0:T(8,128)(2,1)}, bf16[2,64,1024]{2,1,0:T(8,128)(2,1)}, f32[2,64,1024]{2,1,0:T(8,128)}, f32[1,1024]{1,0:T(1,128)}) custom-call(bf16[8,2,8,1152]{3,2,1,0:T(8,128)(2,1)} %bitcast.66, f32[2,8,64,128]{3,2,1,0:T(8,128)} %get-tuple-element.24.weight_ref, bf16[8,2,8,1024]{3,2,1,0:T(8,128)(2,1)} %bitcast.85, ...), custom_call_target="tpu_custom_call" | custom-call | flops 67108864 | bytes 2928640 | tf_op jit(solution)/shard_map/pallas_call | solution.py:37
  47.2 4.8 %shard_map.197 = (bf16[8,2,8,1280]{3,2,1,0:T(8,128)(2,1)}, f32[3,16]{1,0:T(4,128)}) custom-call(bf16[8,2,8,1152]{3,2,1,0:T(8,128)(2,1)} %bitcast.67, f32[2,8,64,128]{3,2,1,0:T(8,128)} %get-tuple-element.26.decay_ref, f32[2,8,64,128]{3,2,1,0:T(8,128)} %get-tuple-element.24.weight_ref, f32[2,64,1024]{2,1,0:T(8,128)} %get-tuple-element.27.intra_ref, ...), custom_call_target="tpu_custom_call" | custom-call | flops 134217728 | bytes 4194304 | tf_op jit(solution)/shard_map/pallas_call | solution.py:451
  52.8 5.5 %all-to-all-start.3 = ((bf16[16,8,1280]{2,1,0:T(8,128)(2,1)}), bf16[16,8,1280]{2,1,0:T(8,128)(2,1)S(1)}, u32[]{:S(2)}, u32[]{:S(2)}) async-start(bf16[16,8,1280]{2,1,0:T(8,128)(2,1)} %bitcast.83), calls=%async_computation.3 | async-start | bytes 655360 | tf_op jit(solution)/shard_map/all_to_all | solution.py:366
  58.8 9.8 %all-to-all-done.3 = bf16[16,8,1280]{2,1,0:T(8,128)(2,1)S(1)} async-done(((bf16[16,8,1280]{2,1,0:T(8,128)(2,1)}), bf16[16,8,1280]{2,1,0:T(8,128)(2,1)S(1)}, u32[]{:S(2)}, u32[]{:S(2)}) %all-to-all-start.3) | async-done | bytes 327712 | tf_op jit(solution)/shard_map/all_to_all | solution.py:366
  69.4 2.6 %shard_map.198 = (bf16[2,8,8,1152]{3,2,1,0:T(8,128)(2,1)}, f32[10,1152]{1,0:T(8,128)}) custom-call(bf16[2,8,8,1280]{3,2,1,0:T(8,128)(2,1)} %bitcast.64, f32[2,8,8,1152]{3,2,1,0:T(8,128)} %get-tuple-element.30.slope_ref, bf16[8,8,1152]{2,1,0:T(8,128)(2,1)} %copy-done.13, bf16[2,8,8,1152]{3,2,1,0:T(8,128)(2,1)} %bitcast.69, bf16[8,8,1152]{2,1,0:T(8,128)(2,1)} %copy-done.12), custom_call_target="tpu_custom_call" | custom-call | flops 1048576 | bytes 1848320 | tf_op jit(solution)/shard_map/pallas_call | solution.py:37
  72.0 0.9 reshape.149
  73.6 7.4 %all-to-all-start.6 = ((f32[128,1,128]{2,1,0:T(1,128)}), f32[128,1,128]{2,1,0:T(1,128)S(1)}, u32[]{:S(2)}, u32[]{:S(2)}) async-start(f32[128,1,128]{2,1,0:T(1,128)} %bitcast.31), calls=%async_computation.6 | async-start | bytes 131072 | tf_op jit(solution)/shard_map/all_to_all | solution.py:366
  81.0 1.7 slice_bitcast_fusion.4
  82.7 1.4 collective-permute-start.3
  84.1 3.7 %collective-permute-start.2 = (bf16[8,8,1152]{2,1,0:T(8,128)(2,1)}, bf16[8,8,1152]{2,1,0:T(8,128)(2,1)}, u32[]{:S(2)}, u32[]{:S(2)}) collective-permute-start(bf16[8,8,1152]{2,1,0:T(8,128)(2,1)} %get-tuple-element.36), channel_id=1, source_target_pairs={{0,1},{1,2},{2,3},{3,4},{4,5},{5,6},{6,7},{7,8},{8,9},{9,10},{10,1... | collective-permute-start | bytes 442376 | tf_op jit(solution)/shard_map/ppermute | solution.py:485
  87.8 2.6 %all-to-all-done.6 = f32[128,1,128]{2,1,0:T(1,128)S(1)} async-done(((f32[128,1,128]{2,1,0:T(1,128)}), f32[128,1,128]{2,1,0:T(1,128)S(1)}, u32[]{:S(2)}, u32[]{:S(2)}) %all-to-all-start.6) | async-done | bytes 65568 | tf_op jit(solution)/shard_map/all_to_all | solution.py:366
  91.1 9.4 %all-to-all-start.7 = ((f32[128,1,128]{2,1,0:T(1,128)}), f32[128,1,128]{2,1,0:T(1,128)S(1)}, u32[]{:S(2)}, u32[]{:S(2)}) async-start(f32[128,1,128]{2,1,0:T(1,128)} %broadcast_in_dim.19), calls=%async_computation.7 | async-start | bytes 131072 | tf_op jit(solution)/shard_map/all_to_all | solution.py:366
  100.5 0.8 maximum_bitcast_fusion
  101.4 8.6 %all-to-all-done.7 = f32[128,1,128]{2,1,0:T(1,128)S(1)} async-done(((f32[128,1,128]{2,1,0:T(1,128)}), f32[128,1,128]{2,1,0:T(1,128)S(1)}, u32[]{:S(2)}, u32[]{:S(2)}) %all-to-all-start.7) | async-done | bytes 65568 | tf_op jit(solution)/shard_map/all_to_all | solution.py:366
  109.9 3.5 %all-to-all-start.2 = ((bf16[16,8,2048]{2,1,0:T(8,128)(2,1)}), bf16[16,8,2048]{2,1,0:T(8,128)(2,1)S(1)}, u32[]{:S(2)}, u32[]{:S(2)}) async-start(bf16[16,8,2048]{2,1,0:T(8,128)(2,1)} %maximum_bitcast_fusion), calls=%async_computation.2 | async-start | bytes 1048576 | tf_op jit(solution)/shard_map/all_to_all | solution.py:366
  113.4 2.5 %shard_map.199 = bf16[2,8,8,1280]{3,2,1,0:T(8,128)(2,1)} custom-call(bf16[8,8,1152]{2,1,0:T(8,128)(2,1)} %collective-permute-done.2.low_ref, bf16[8,8,1152]{2,1,0:T(8,128)(2,1)} %collective-permute-done.3.high_ref, bf16[2,8,8,1280]{3,2,1,0:T(8,128)(2,1)} %bitcast.65, f32[2,8,8,1152]{3,2,1,0:T(8,128)} %get-tuple-element.30.slope_ref, ...), custom_call_target="tpu_custom_call" | custom-call | flops 1048576 | bytes 1581568 | tf_op jit(solution)/shard_map/pallas_call | solution.py:37
  116.4 1.7 collective-permute-done.6.refs_2_
  118.9 5.3 %shard_map.201 = bf16[64,8,1280]{2,1,0:T(8,128)(2,1)} custom-call(s32[1,1]{1,0:T(1,128)} %bitcast.29.refs_0_, bf16[128,1024]{1,0:T(8,128)(2,1)} %bitcast.79, bf16[128,1024]{1,0:T(8,128)(2,1)} %copy-done.15, bf16[128,1280]{1,0:T(8,128)(2,1)} %bitcast.62, bf16[128,1280]{1,0:T(8,128)(2,1)} %copy-done.14), custom_call_target="tpu_custom_call" | custom-call | flops 671088640 | bytes 2490372 | tf_op jit(solution)/shard_map/pallas_call | solution.py:37
  124.2 1.1 all-to-all-done.2
  126.1 7.6 %all-to-all-start.5 = ((bf16[64,8,1280]{2,1,0:T(8,128)(2,1)}), bf16[64,8,1280]{2,1,0:T(8,128)(2,1)S(1)}, u32[]{:S(2)}, u32[]{:S(2)}) async-start(bf16[64,8,1280]{2,1,0:T(8,128)(2,1)} %shard_map.201), calls=%async_computation.5 | async-start | bytes 2621440 | tf_op jit(solution)/shard_map/all_to_all | solution.py:366
  134.3 1.7 collective-permute-done.4.refs_2_
  136.8 8.2 %shard_map.200 = bf16[64,8,2048]{2,1,0:T(8,128)(2,1)} custom-call(s32[1,1]{1,0:T(1,128)} %bitcast.29.refs_0_, bf16[128,2048]{1,0:T(8,128)(2,1)} %bitcast.60, bf16[128,2048]{1,0:T(8,128)(2,1)} %collective-permute-done.4.refs_2_, bf16[128,2048]{1,0:T(8,128)(2,1)} %bitcast.71, bf16[128,2048]{1,0:T(8,128)(2,1)} %collective-permute-done.5.refs_4_), custom_call_target="tpu_custom_call" | custom-call | flops 1073741824 | bytes 4194308 | tf_op jit(solution)/shard_map/pallas_call | solution.py:37
  145.0 10.2 %all-to-all-done.5 = bf16[64,8,1280]{2,1,0:T(8,128)(2,1)S(1)} async-done(((bf16[64,8,1280]{2,1,0:T(8,128)(2,1)}), bf16[64,8,1280]{2,1,0:T(8,128)(2,1)S(1)}, u32[]{:S(2)}, u32[]{:S(2)}) %all-to-all-start.5) | async-done | bytes 1310752 | tf_op jit(solution)/shard_map/all_to_all | solution.py:366
  155.2 6.0 %all-to-all-start.4 = ((bf16[64,8,2048]{2,1,0:T(8,128)(2,1)}), bf16[64,8,2048]{2,1,0:T(8,128)(2,1)}, u32[]{:S(2)}, u32[]{:S(2)}) async-start(bf16[64,8,2048]{2,1,0:T(8,128)(2,1)} %shard_map.200), calls=%async_computation.4 | async-start | bytes 4194304 | tf_op jit(solution)/shard_map/all_to_all | solution.py:366
  161.2 0.8 copy.60
  162.1 3.3 %slice.75 = bf16[1024,1152]{1,0:T(8,128)(2,1)} slice(bf16[1024,2176]{1,0:T(8,128)(2,1)} %param.12), slice={[0:1024], [1024:2176]} | slice | bytes 4718592 | tf_op jit(solution)/shard_map/slice | solution.py:402
  166.2 5.1 %concatenate.17 = bf16[1024,1280]{1,0:T(8,128)(2,1)} concatenate(bf16[1024,1152]{1,0:T(8,128)(2,1)} %slice.75, bf16[1024,16]{1,0:T(8,128)(2,1)} %copy.60, bf16[1024,112]{1,0:T(8,128)(2,1)} %broadcast_in_dim.17), dimensions={1} | concatenate | bytes 5242880 | tf_op jit(solution)/shard_map/concatenate | solution.py:501
  173.8 1.1 slice.105
  175.0 0.9 copy.66
  175.8 2.5 %fusion = f32[128,1024]{1,0:T(8,128)S(1)} fusion(bf16[1024,2176]{1,0:T(8,128)(2,1)} %param.12, bf16[16,8,2048]{2,1,0:T(8,128)(2,1)} %copy-done.8), kind=kOutput, calls=%fused_computation.3 | convolution fusion | flops 268435456 | bytes 2883584 | tf_op jit(solution)/shard_map/dot_general | solution.py:47
  178.4 1.0 fusion.4
  179.3 0.9 copy.65
  181.0 9.2 %all-to-all-done.4 = bf16[64,8,2048]{2,1,0:T(8,128)(2,1)} async-done(((bf16[64,8,2048]{2,1,0:T(8,128)(2,1)}), bf16[64,8,2048]{2,1,0:T(8,128)(2,1)}, u32[]{:S(2)}, u32[]{:S(2)}) %all-to-all-start.4) | async-done | bytes 2097184 | tf_op jit(solution)/shard_map/all_to_all | solution.py:366
  190.2 1.9 convert_reduce_fusion
  (81 shorter events, 17.5 us)
Async XLA Ops:
  0.6 33.6 %copy-start = (bf16[1024,1024]{1,0:T(8,128)(2,1)S(1)}, bf16[1024,1024]{1,0:T(8,128)(2,1)}, u32[]{:S(2)}) copy-start(bf16[1024,1024]{1,0:T(8,128)(2,1)} %param.20) | copy-start | bytes 6291460
  0.7 11.0 %copy-start.9 = (bf16[8,2,8,1024]{3,2,1,0:T(8,128)(2,1)S(1)}, bf16[8,2,8,1024]{3,2,1,0:T(8,128)(2,1)}, u32[]{:S(2)}) copy-start(bf16[8,2,8,1024]{3,2,1,0:T(8,128)(2,1)} %param.11) | copy-start | bytes 786436
  3.9 21.5 %all-to-all-start.1 = ((bf16[16,8,2048]{2,1,0:T(8,128)(2,1)}), bf16[16,8,2048]{2,1,0:T(8,128)(2,1)S(1)}, u32[]{:S(2)}, u32[]{:S(2)}) async-start(bf16[16,8,2048]{2,1,0:T(8,128)(2,1)} %pad_maximum_fusion), calls=%async_computation.1 | async-start | bytes 1048576 | tf_op jit(solution)/shard_map/all_to_all | solution.py:366
  11.8 0.7 copy-start.10
  11.8 7.3 %copy-start.18 = (f32[1152]{0:T(1024)S(1)}, f32[1152]{0:T(1024)}, u32[]{:S(2)}) copy-start(f32[1152]{0:T(1024)} %param.17) | copy-start | bytes 13828
  11.8 7.9 %copy-start.20 = (f32[16]{0:T(128)S(1)}, f32[16]{0:T(128)}, u32[]{:S(2)}) copy-start(f32[16]{0:T(128)} %param.18) | copy-start | bytes 196
  12.5 20.1 %copy-start.16 = (bf16[1024,16]{0,1:T(8,128)(2,1)S(1)}, bf16[1024,16]{0,1:T(8,128)(2,1)}, u32[]{:S(2)}) copy-start(bf16[1024,16]{0,1:T(8,128)(2,1)} %param.13) | copy-start | bytes 98308
  12.5 20.1 %copy-start.21 = (f32[16]{0:T(128)S(1)}, f32[16]{0:T(128)}, u32[]{:S(2)}) copy-start(f32[16]{0:T(128)} %param.14) | copy-start | bytes 196
  14.7 7.2 %copy-start.6 = (bf16[128,1152]{1,0:T(8,128)(2,1)}, bf16[128,1152]{1,0:T(8,128)(2,1)S(1)}, u32[]{:S(2)}) copy-start(bf16[128,1152]{1,0:T(8,128)(2,1)S(1)} %convolution_convert_fusion) | copy-start | bytes 884740
  14.7 7.2 %collective-permute-start.1 = (bf16[8,8,1152]{2,1,0:T(8,128)(2,1)S(1)}, bf16[8,8,1152]{2,1,0:T(8,128)(2,1)S(1)}, u32[]{:S(2)}, u32[]{:S(2)}) collective-permute-start(bf16[8,8,1152]{2,1,0:T(8,128)(2,1)S(1)} %get-tuple-element.37), channel_id=1, source_target_pairs={{1,0},{2,1},{3,2},{4,3},{5,4},{6,5},{7,6},{8,7},{9,8},{10,9},{11,1... | collective-permute-start | bytes 442376 | tf_op jit(solution)/shard_map/ppermute | solution.py:409
  16.0 5.9 %collective-permute-start = (bf16[8,8,1152]{2,1,0:T(8,128)(2,1)S(1)}, bf16[8,8,1152]{2,1,0:T(8,128)(2,1)S(1)}, u32[]{:S(2)}, u32[]{:S(2)}) collective-permute-start(bf16[8,8,1152]{2,1,0:T(8,128)(2,1)S(1)} %get-tuple-element.38), channel_id=1, source_target_pairs={{0,1},{1,2},{2,3},{3,4},{4,5},{5,6},{6,7},{7,8},{8,9},{9,10},{10,1... | collective-permute-start | bytes 442376 | tf_op jit(solution)/shard_map/ppermute | solution.py:408
  21.9 0.7 copy-start.12
  21.9 0.7 copy-start.13
  25.4 16.0 %copy-start.2 = (bf16[16,8,2048]{2,1,0:T(8,128)(2,1)}, bf16[16,8,2048]{2,1,0:T(8,128)(2,1)S(1)}, u32[]{:S(2)}) copy-start(bf16[16,8,2048]{2,1,0:T(8,128)(2,1)S(1)} %all-to-all-done.1) | copy-start | bytes 1572868
  25.4 17.7 %all-to-all-start = ((bf16[16,8,1152]{2,1,0:T(8,128)(2,1)}), bf16[16,8,1152]{2,1,0:T(8,128)(2,1)S(1)}, u32[]{:S(2)}, u32[]{:S(2)}) async-start(bf16[16,8,1152]{2,1,0:T(8,128)(2,1)} %bitcast.84), calls=%async_computation | async-start | bytes 589824 | tf_op jit(solution)/shard_map/all_to_all | solution.py:366
  43.1 0.7 copy-start.5
  47.2 11.1 %copy-start.7 = (bf16[8,2,8,2048]{3,2,1,0:T(8,128)(2,1)S(1)}, bf16[8,2,8,2048]{3,2,1,0:T(8,128)(2,1)}, u32[]{:S(2)}) copy-start(bf16[8,2,8,2048]{3,2,1,0:T(8,128)(2,1)} %get-tuple-element.25) | copy-start | bytes 1572868
  52.8 15.8 %all-to-all-start.3 = ((bf16[16,8,1280]{2,1,0:T(8,128)(2,1)}), bf16[16,8,1280]{2,1,0:T(8,128)(2,1)S(1)}, u32[]{:S(2)}, u32[]{:S(2)}) async-start(bf16[16,8,1280]{2,1,0:T(8,128)(2,1)} %bitcast.83), calls=%async_computation.3 | async-start | bytes 655360 | tf_op jit(solution)/shard_map/all_to_all | solution.py:366
  58.4 14.5 %copy-start.19 = (f32[1,1024]{1,0:T(1,128)S(1)}, f32[1,1024]{1,0:T(1,128)}, u32[]{:S(2)}) copy-start(f32[1,1024]{1,0:T(1,128)} %get-tuple-element.33) | copy-start | bytes 12292
  68.6 0.7 copy-start.4
  73.6 16.8 %all-to-all-start.6 = ((f32[128,1,128]{2,1,0:T(1,128)}), f32[128,1,128]{2,1,0:T(1,128)S(1)}, u32[]{:S(2)}, u32[]{:S(2)}) async-start(f32[128,1,128]{2,1,0:T(1,128)} %bitcast.31), calls=%async_computation.6 | async-start | bytes 131072 | tf_op jit(solution)/shard_map/all_to_all | solution.py:366
  82.7 33.2 %copy-start.11 = (bf16[2,8,8,1024]{3,2,1,0:T(8,128)(2,1)S(1)}, bf16[2,8,8,1024]{3,2,1,0:T(8,128)(2,1)}, u32[]{:S(2)}) copy-start(bf16[2,8,8,1024]{3,2,1,0:T(8,128)(2,1)} %copy-done.10) | copy-start | bytes 786436
  82.7 30.7 %collective-permute-start.3 = (bf16[8,8,1152]{2,1,0:T(8,128)(2,1)}, bf16[8,8,1152]{2,1,0:T(8,128)(2,1)}, u32[]{:S(2)}, u32[]{:S(2)}) collective-permute-start(bf16[8,8,1152]{2,1,0:T(8,128)(2,1)} %get-tuple-element.35), channel_id=1, source_target_pairs={{1,0},{2,1},{3,2},{4,3},{5,4},{6,5},{7,6},{8,7},{9,8},{10,9},{11,1... | collective-permute-start | bytes 442376 | tf_op jit(solution)/shard_map/ppermute | solution.py:486
  84.1 29.3 %collective-permute-start.2 = (bf16[8,8,1152]{2,1,0:T(8,128)(2,1)}, bf16[8,8,1152]{2,1,0:T(8,128)(2,1)}, u32[]{:S(2)}, u32[]{:S(2)}) collective-permute-start(bf16[8,8,1152]{2,1,0:T(8,128)(2,1)} %get-tuple-element.36), channel_id=1, source_target_pairs={{0,1},{1,2},{2,3},{3,4},{4,5},{5,6},{6,7},{7,8},{8,9},{9,10},{10,1... | collective-permute-start | bytes 442376 | tf_op jit(solution)/shard_map/ppermute | solution.py:485
  91.1 18.8 %all-to-all-start.7 = ((f32[128,1,128]{2,1,0:T(1,128)}), f32[128,1,128]{2,1,0:T(1,128)S(1)}, u32[]{:S(2)}, u32[]{:S(2)}) async-start(f32[128,1,128]{2,1,0:T(1,128)} %broadcast_in_dim.19), calls=%async_computation.7 | async-start | bytes 131072 | tf_op jit(solution)/shard_map/all_to_all | solution.py:366
  109.9 15.4 %all-to-all-start.2 = ((bf16[16,8,2048]{2,1,0:T(8,128)(2,1)}), bf16[16,8,2048]{2,1,0:T(8,128)(2,1)S(1)}, u32[]{:S(2)}, u32[]{:S(2)}) async-start(bf16[16,8,2048]{2,1,0:T(8,128)(2,1)} %maximum_bitcast_fusion), calls=%async_computation.2 | async-start | bytes 1048576 | tf_op jit(solution)/shard_map/all_to_all | solution.py:366
  115.9 2.2 %collective-permute-start.7 = (bf16[128,1280]{1,0:T(8,128)(2,1)}, bf16[128,1280]{1,0:T(8,128)(2,1)S(1)}, u32[]{:S(2)}, u32[]{:S(2)}) collective-permute-start(bf16[128,1280]{1,0:T(8,128)(2,1)} %bitcast.61), channel_id=1, source_target_pairs={{0,1},{1,0},{2,3},{3,2},{4,5},{5,4},{6,7},{7,6},{8,9},{9,8},{10,11... | collective-permute-start | bytes 983048 | tf_op jit(solution)/shard_map/ppermute | solution.py:497
  115.9 2.2 %collective-permute-start.6 = (bf16[128,1024]{1,0:T(8,128)(2,1)S(1)}, bf16[128,1024]{1,0:T(8,128)(2,1)S(1)}, u32[]{:S(2)}, u32[]{:S(2)}) collective-permute-start(bf16[128,1024]{1,0:T(8,128)(2,1)S(1)} %bitcast.80), channel_id=1, source_target_pairs={{0,1},{1,0},{2,3},{3,2},{4,5},{5,4},{6,7},{7,6},{8,9},{9,8},{10,11... | collective-permute-start | bytes 786440 | tf_op jit(solution)/shard_map/ppermute | solution.py:496
  118.1 0.7 copy-start.15
  118.1 0.8 copy-start.14
  125.3 0.8 copy-start.8
  126.1 29.1 %all-to-all-start.5 = ((bf16[64,8,1280]{2,1,0:T(8,128)(2,1)}), bf16[64,8,1280]{2,1,0:T(8,128)(2,1)S(1)}, u32[]{:S(2)}, u32[]{:S(2)}) async-start(bf16[64,8,1280]{2,1,0:T(8,128)(2,1)} %shard_map.201), calls=%async_computation.5 | async-start | bytes 2621440 | tf_op jit(solution)/shard_map/all_to_all | solution.py:366
  133.7 2.3 %collective-permute-start.4 = (bf16[128,2048]{1,0:T(8,128)(2,1)}, bf16[128,2048]{1,0:T(8,128)(2,1)}, u32[]{:S(2)}, u32[]{:S(2)}) collective-permute-start(bf16[128,2048]{1,0:T(8,128)(2,1)} %bitcast.59), channel_id=1, source_target_pairs={{0,1},{1,0},{2,3},{3,2},{4,5},{5,4},{6,7},{7,6},{8,9},{9,8},{10,11... | collective-permute-start | bytes 1572872 | tf_op jit(solution)/shard_map/ppermute | solution.py:471
  133.8 3.0 %collective-permute-start.5 = (bf16[128,2048]{1,0:T(8,128)(2,1)}, bf16[128,2048]{1,0:T(8,128)(2,1)}, u32[]{:S(2)}, u32[]{:S(2)}) collective-permute-start(bf16[128,2048]{1,0:T(8,128)(2,1)} %bitcast.70), channel_id=1, source_target_pairs={{0,1},{1,0},{2,3},{3,2},{4,5},{5,4},{6,7},{7,6},{8,9},{9,8},{10,11... | collective-permute-start | bytes 1572872 | tf_op jit(solution)/shard_map/ppermute | solution.py:472
  145.0 16.3 %copy-start.17 = (bf16[1024,16]{0,1:T(8,128)(2,1)S(1)}, bf16[1024,16]{0,1:T(8,128)(2,1)}, u32[]{:S(2)}) copy-start(bf16[1024,16]{0,1:T(8,128)(2,1)} %param.13) | copy-start | bytes 98308
  155.2 35.0 %all-to-all-start.4 = ((bf16[64,8,2048]{2,1,0:T(8,128)(2,1)}), bf16[64,8,2048]{2,1,0:T(8,128)(2,1)}, u32[]{:S(2)}, u32[]{:S(2)}) async-start(bf16[64,8,2048]{2,1,0:T(8,128)(2,1)} %shard_map.200), calls=%async_computation.4 | async-start | bytes 4194304 | tf_op jit(solution)/shard_map/all_to_all | solution.py:366
  173.8 4.5 %copy-start.1 = (bf16[1024,1280]{1,0:T(8,128)(2,1)S(1)}, bf16[1024,1280]{1,0:T(8,128)(2,1)}, u32[]{:S(2)}) copy-start(bf16[1024,1280]{1,0:T(8,128)(2,1)} %concatenate.17) | copy-start | bytes 7864324
  173.8 4.5 %copy-start.3 = (bf16[2,8,8,1280]{3,2,1,0:T(8,128)(2,1)S(1)}, bf16[2,8,8,1280]{3,2,1,0:T(8,128)(2,1)}, u32[]{:S(2)}) copy-start(bf16[2,8,8,1280]{3,2,1,0:T(8,128)(2,1)} %shard_map.199) | copy-start | bytes 983044

commit v2 on v1

v2 whole, which is shorter than its diff:
```python
import jax
import jax.numpy as jnp
from jax import lax
from jax.experimental import pallas as pl
from jax.experimental.pallas import tpu as pltpu
from jax.sharding import Mesh
from jax.sharding import PartitionSpec as P

SPACE = ("space_0", "space_1", "space_2")
TM = ("tm_0", "tm_1")
TM_SPACE = ("tm_0", "tm_1", "space_0", "space_1", "space_2")
CHIPS = ("tm_0", "tm_1", "space_0", "space_1")
CORE = "space_2"

HIGH = lax.Precision.HIGHEST
NORM_EPS = 1e-05
F32 = jnp.float32
BF16 = jnp.bfloat16
VMEM = pl.BlockSpec(memory_space=pltpu.VMEM)
SMEM = pl.BlockSpec(memory_space=pltpu.SMEM)
ANY = pl.BlockSpec(memory_space=pl.ANY)
LANES = 128


def shape_of(dims, dtype):
    return jax.ShapeDtypeStruct(dims, dtype)


def iota(dims, axis):
    return lax.broadcasted_iota(jnp.int32, dims, axis)


def call(body, out_shape, *args, flops=1 << 20, special=None, scratch=(), room=16):
    specs = [(special or {}).get(k, VMEM) for k in range(len(args))]
    outs = jax.tree.map(lambda _: VMEM, out_shape)
    moved = sum(a.size * a.dtype.itemsize for a in args)
    moved += sum(o.size * o.dtype.itemsize for o in jax.tree.leaves(out_shape))
    return pl.pallas_call(
        body,
        out_shape=out_shape,
        in_specs=specs,
        out_specs=outs,
        scratch_shapes=scratch,
        compiler_params=pltpu.CompilerParams(vmem_limit_bytes=room << 20),
        cost_estimate=pl.CostEstimate(flops=flops, bytes_accessed=moved, transcendentals=0),
    )(*args)


def dot_nt(a, b, precision=None):
    return lax.dot_general(
        a, b, (((1,), (1,)), ((), ())), precision=precision, preferred_element_type=F32
    )


def dot_tn(a, b, precision=None):
    return lax.dot_general(
        a, b, (((0,), (0,)), ((), ())), precision=precision, preferred_element_type=F32
    )


def dot_nn(a, b, precision=None):
    return jnp.dot(a, b, precision=precision, preferred_element_type=F32)


def sigmoid(x):
    return 1.0 / (1.0 + jnp.exp(-x))


def conv_body(
    low_ref, mid_ref, high_ref, kernel_ref, bias_ref, act_ref, cot_ref, send_ref, slope_ref
):
    rows, cols = mid_ref.shape[:2]
    channels = mid_ref.shape[3]
    for r in range(rows):
        for c in range(cols):
            send_ref[r, c, :, channels : channels + act_ref.shape[3]] = act_ref[r, c]
            send_ref[r, c, :, channels + act_ref.shape[3] :] = cot_ref[r, c]

    def chunk(k, carry):
        lanes = pl.ds(pl.multiple_of(k * LANES, LANES), LANES)
        taps = [kernel_ref[t : t + 1, lanes] for t in range(9)]
        bias = bias_ref[0:1, lanes]
        grid = [
            [low_ref[c, :, lanes].astype(F32) for c in range(cols)],
            *[[mid_ref[r, c, :, lanes].astype(F32) for c in range(cols)] for r in range(rows)],
            [high_ref[c, :, lanes].astype(F32) for c in range(cols)],
        ]
        for r in range(rows):
            for c in range(cols):
                total = None
                for i in range(3):
                    for j in range(3):
                        if 0 <= c + j - 1 < cols:
                            term = taps[3 * i + j] * grid[r + i][c + j - 1]
                            total = term if total is None else total + term
                before = total + bias
                gate = sigmoid(before)
                send_ref[r, c, :, lanes] = (before * gate).astype(BF16)
                slope_ref[r, c, :, lanes] = gate * (1.0 + before * (1.0 - gate))
        return carry

    lax.fori_loop(0, channels // LANES, chunk, 0)


def conv_grad_body(
    moved_ref, slope_ref, low_ref, mid_ref, high_ref, norm_ref, small_ref, before_ref, sums_ref
):
    rows, cols = mid_ref.shape[:2]
    channels = mid_ref.shape[3]
    heads = small_ref.shape[1]

    def chunk(k, carry):
        lanes = pl.ds(pl.multiple_of(k * LANES, LANES), LANES)
        grid = [
            [low_ref[c, :, lanes].astype(F32) for c in range(cols)],
            *[[mid_ref[r, c, :, lanes].astype(F32) for c in range(cols)] for r in range(rows)],
            [high_ref[c, :, lanes].astype(F32) for c in range(cols)],
        ]
        sums = [None] * 10
        for r in range(rows):
            for c in range(cols):
                d_before = moved_ref[r, c, :, lanes].astype(F32) * slope_ref[r, c, :, lanes]
                before_ref[r, c, :, lanes] = d_before.astype(BF16)
                for i in range(3):
                    for j in range(3):
                        if 0 <= c + j - 1 < cols:
                            term = d_before * grid[r + i][c + j - 1]
                            t = 3 * i + j
                            sums[t] = term if sums[t] is None else sums[t] + term
                sums[9] = d_before if sums[9] is None else sums[9] + d_before
        for t in range(10):
            sums_ref[t : t + 1, lanes] = jnp.sum(sums[t], axis=0, keepdims=True)
        return carry

    lax.fori_loop(0, channels // LANES, chunk, 0)
    inner = norm_ref.shape[1]
    sums_ref[10:11, :inner] = norm_ref[...]
    sums_ref[10:11, inner:] = jnp.zeros((1, channels - inner), F32)
    sums_ref[11:16] = jnp.zeros((5, channels), F32)
    for k in range(3):
        sums_ref[11:12, k * LANES : k * LANES + heads] = small_ref[k : k + 1]


def conv_spread_body(low_ref, high_ref, moved_ref, slope_ref, kernel_ref, out_ref):
    rows, cols = moved_ref.shape[:2]
    channels = slope_ref.shape[3]

    def chunk(k, carry):
        lanes = pl.ds(pl.multiple_of(k * LANES, LANES), LANES)
        taps = [kernel_ref[t : t + 1, lanes] for t in range(9)]
        grid = [
            [low_ref[c, :, lanes].astype(F32) for c in range(cols)],
            *[
                [
                    moved_ref[r, c, :, lanes].astype(F32) * slope_ref[r, c, :, lanes]
                    for c in range(cols)
                ]
                for r in range(rows)
            ],
            [high_ref[c, :, lanes].astype(F32) for c in range(cols)],
        ]
        for r in range(rows):
            for c in range(cols):
                total = None
                for i in range(3):
                    for j in range(3):
                        if 0 <= c + 1 - j < cols:
                            term = taps[3 * i + j] * grid[r + 2 - i][c + 1 - j]
                            total = term if total is None else total + term
                out_ref[r, c, :, lanes] = total.astype(BF16)
        return carry

    lax.fori_loop(0, channels // LANES, chunk, 0)
    tail = slice(channels, out_ref.shape[3])
    for r in range(rows):
        for c in range(cols):
            out_ref[r, c, :, tail] = moved_ref[r, c, :, tail]


def head_select(heads, width):
    dims = (heads, heads * width)
    return (iota(dims, 1) // width == iota(dims, 0)).astype(F32)


def turn_body(core_ref, cot_ref, act_ref, mine_ref, other_ref):
    core = core_ref[0, 0]
    per = cot_ref.shape[1] // LANES
    for k in range(2 * per):
        source = cot_ref if k < per else act_ref
        at = (k % per) * LANES
        block = source[:, at : at + LANES].astype(F32).T
        split = block.reshape(LANES // 16, 2, 8, block.shape[1])
        even = split[:, 0].reshape(LANES // 2, block.shape[1]).astype(BF16)
        odd = split[:, 1].reshape(LANES // 2, block.shape[1]).astype(BF16)
        rows = slice(k * LANES // 2, (k + 1) * LANES // 2)
        mine_ref[rows] = jnp.where(core == 0, even, odd)
        other_ref[rows] = jnp.where(core == 0, odd, even)


def decays(steps, rate, decay_ref, weight_ref, tok):
    frames, heads = steps.shape
    pairs = heads // 2
    wide = 2 * frames
    lower = (iota((frames, frames), 0) >= iota((frames, frames), 1)).astype(F32)
    row2 = iota((frames, wide), 0)
    lane2 = iota((frames, wide), 1)
    inner2 = jnp.where(lane2 < frames, lane2, lane2 - frames)
    upper2 = (row2 <= inner2).astype(F32)
    eye2 = (row2 == inner2).astype(F32)
    causal = row2 >= inner2
    first = iota((1, wide), 1) < frames
    decay = steps * rate
    running = dot_nn(lower, decay, HIGH)
    running_t = dot_tn(decay, upper2, HIGH)
    steps_t = dot_tn(steps, eye2, HIGH)
    spread_cols = dot_nn(running, head_select(heads, frames), HIGH)
    for j in range(pairs):
        row = jnp.where(first, running_t[2 * j : 2 * j + 1], running_t[2 * j + 1 : 2 * j + 2])
        step_row = jnp.where(first, steps_t[2 * j : 2 * j + 1], steps_t[2 * j + 1 : 2 * j + 2])
        spread = spread_cols[:, j * wide : (j + 1) * wide] - row
        kept = jnp.where(causal, jnp.exp(-jnp.where(causal, spread, 0.0)), 0.0)
        decay_ref[tok, j] = kept
        weight_ref[tok, j] = kept * step_row


def unpack(tok_values, frames, inner):
    lane = iota((frames, LANES), 1)
    left = lane < LANES // 2
    mixed = tok_values[:, inner : inner + LANES]
    swapped = pltpu.roll(mixed, LANES // 2, 1)
    b_left = jnp.where(left, mixed, 0.0)
    c_left = jnp.where(left, swapped, 0.0)
    b_right = jnp.where(left, 0.0, swapped)
    return left, b_left, c_left, b_right


def score(b_left, c_left):
    both = jnp.concatenate([b_left, b_left], axis=0).astype(BF16)
    return dot_nt(c_left.astype(BF16), both)


def block_diag(pair, left):
    zero = jnp.zeros_like(pair)
    return jnp.concatenate([jnp.where(left, pair, zero), jnp.where(left, zero, pair)], axis=0)


def rollout_body(
    act_ref,
    rate_ref,
    skip_ref,
    gain_ref,
    step_proj_ref,
    step_bias_ref,
    in_proj_ref,
    out_proj_ref,
    out_ref,
    part_ref,
    small_ref,
    decay_ref,
    weight_ref,
    intra_ref,
    d_ssd_ref,
    pulled_ref,
    gate_proj_ref,
    cot_proj_ref,
    gate_ref,
    cot_ref,
    sems,
):
    fetches = (
        pltpu.make_async_copy(in_proj_ref.at[:, : gate_proj_ref.shape[1]], gate_proj_ref, sems.at[0]),
        pltpu.make_async_copy(out_proj_ref, cot_proj_ref, sems.at[1]),
    )
    for fetch in fetches:
        fetch.start()
    tokens = act_ref.shape[1]
    blocks, per = act_ref.shape[0], act_ref.shape[2]
    frames = blocks * per
    heads = rate_ref.shape[1]
    inner = skip_ref.shape[1]
    pairs = heads // 2
    packed = inner + LANES
    model = out_proj_ref.shape[1]
    at_gate = packed + LANES
    at_cot = at_gate + inner
    select = head_select(heads, inner // heads)
    dims = (frames, frames)
    upper = (iota(dims, 0) <= iota(dims, 1)).astype(F32)
    gain = gain_ref[...]
    rate = rate_ref[...]
    sums = {}

    def add(key, term):
        sums[key] = sums[key] + term if key in sums else term

    def read(tok, start, size):
        return act_ref[:, tok, :, start : start + size].astype(F32).reshape(frames, size)

    def write(tok, start, value):
        size = value.shape[1]
        out_ref[:, tok, :, start : start + size] = value.reshape(blocks, per, size).astype(BF16)

    every = [
        jnp.concatenate(
            [act_ref[:, tok, :, start : start + model].astype(F32).reshape(frames, model) for tok in range(tokens)],
            axis=0,
        ).astype(BF16)
        for start in (packed, packed + model)
    ]
    raw = dot_nn(every[0], step_proj_ref[...]) + step_bias_ref[...]
    small = jnp.exp(-jnp.abs(raw))
    grown = 1.0 + small
    flat = grown == 1.0
    safe = jnp.where(flat, 1.0, grown - 1.0)
    log_part = jnp.where(flat, small, jnp.log(grown) * (small / safe))
    all_steps = (jnp.maximum(raw, 0.0) + log_part).astype(BF16).astype(F32)
    tok_steps = [all_steps[tok * frames : (tok + 1) * frames] for tok in range(tokens)]
    for tok in range(tokens):
        decays(tok_steps[tok], rate, decay_ref, weight_ref, tok)
        values = read(tok, 0, packed)
        left, b_left, c_left, _ = unpack(values, frames, inner)
        scores = score(b_left, c_left)
        for j in range(pairs):
            lanes = slice(j * LANES, (j + 1) * LANES)
            pair = values[:, lanes]
            mix = weight_ref[tok, j] * scores
            coarse = mix.astype(BF16)
            fine = (mix - coarse.astype(F32)).astype(BF16)
            diag = block_diag(pair, left).astype(BF16)
            intra_ref[tok, :, lanes] = dot_nn(coarse, diag) + dot_nn(fine, diag)
    fetches[0].wait()
    gate_ref[...] = dot_nn(every[0], gate_proj_ref[...]).astype(BF16)
    fetches[1].wait()
    cot_ref[...] = dot_nt(every[1], cot_proj_ref[...])

    for tok in range(tokens):
        values = read(tok, 0, inner)
        rows = slice(tok * frames, (tok + 1) * frames)
        ssd = (intra_ref[tok] + skip_ref[...] * values).astype(BF16).astype(F32)
        gate = gate_ref[rows].astype(F32)
        squashed = sigmoid(gate)
        opened = gate * squashed
        gated = ssd * opened
        scale = lax.rsqrt(jnp.mean(gated * gated, axis=-1, keepdims=True) + NORM_EPS)
        unit = gated * scale
        cot = cot_ref[rows]
        add("norm", jnp.sum(cot * unit, axis=0, keepdims=True))
        pulled = cot * gain
        along = jnp.mean(pulled * unit, axis=-1, keepdims=True)
        d_gated = scale * (pulled - unit * along)
        d_ssd_ref[tok] = (d_gated * opened).astype(BF16)
        write(tok, at_gate, unit * gain)
        write(tok, at_cot, d_gated * ssd * (squashed * (1.0 + gate * (1.0 - squashed))))
    part_ref[...] = sums["norm"]

    for tok in range(tokens):
        values = read(tok, 0, packed)
        left, b_left, c_left, b_right = unpack(values, frames, inner)
        scores = score(b_left, c_left)
        d_scores = jnp.zeros((frames, LANES), F32)
        for j in range(pairs):
            lanes = slice(j * LANES, (j + 1) * LANES)
            pair = values[:, lanes]
            d_pair = d_ssd_ref[tok, :, lanes]
            diag = block_diag(pair, left).astype(BF16)
            d_scores = d_scores + dot_nt(d_pair, diag) * weight_ref[tok, j]
            mix = decay_ref[tok, j] * scores
            coarse = mix.astype(BF16)
            fine = (mix - coarse.astype(F32)).astype(BF16)
            wide = dot_tn(coarse, d_pair) + dot_tn(fine, d_pair)
            pulled_ref[:, lanes] = jnp.where(left, wide[:frames], wide[frames:])
        u = values[:, :inner]
        dy = d_ssd_ref[tok].astype(F32)
        pulled = pulled_ref[...]
        steps = tok_steps[tok]
        write(tok, 0, dot_nn(steps, select, HIGH) * pulled + skip_ref[...] * dy)
        q = dot_nt(dy * intra_ref[tok], select, HIGH)
        r = dot_nt(u * pulled, select, HIGH)
        add("skip", dot_nt(jnp.sum(dy * u, axis=0, keepdims=True), select, HIGH))
        d_decay = dot_nn(upper, steps * r - q, HIGH)
        add("rate", jnp.sum(d_decay * steps, axis=0, keepdims=True))
        d_steps = (r + rate * d_decay).astype(BF16).astype(F32)
        d_raw = d_steps * sigmoid(raw[tok * frames : (tok + 1) * frames])
        add("bias", jnp.sum(d_raw, axis=0, keepdims=True))
        folded = d_scores + pltpu.roll(d_scores, LANES // 2, 1)
        folded = jnp.where(left, folded, 0.0).astype(BF16)
        stacked = jnp.concatenate([b_right, jnp.zeros_like(b_right)], axis=0).astype(BF16)
        write(tok, inner, dot_nn(folded, stacked) + dot_tn(folded, c_left.astype(BF16))[:frames])
        write(
            tok,
            packed,
            jnp.concatenate([d_raw, jnp.zeros((frames, LANES - heads), F32)], axis=1),
        )
    for k, key in enumerate(("bias", "rate", "skip")):
        small_ref[k : k + 1, :] = sums[key]


def outer_body(left_ref, left2_ref, home_ref, home2_ref, late_ref, late2_ref, out_ref):
    groups, eight, cols = out_ref.shape
    rows = groups * eight
    width = late_ref.shape[1]
    inner = (cols - width) // 2
    step = 2 * LANES
    parts = (
        (0, home_ref, home2_ref, width, 0, inner),
        (1, home_ref, home2_ref, width + inner, inner, inner),
        (1, late_ref, late2_ref, 0, 2 * inner, width),
    )
    for side, right_ref, right2_ref, start, at, size in parts:
        lanes = slice(start, start + size)
        right = jnp.concatenate([right_ref[:, lanes], right2_ref[:, lanes]], axis=0)
        for k in range(rows // step):
            block = slice(side * rows + k * step, side * rows + (k + 1) * step)
            left = jnp.concatenate([left_ref[block], left2_ref[block]], axis=1)
            total = dot_nn(left, right).reshape(step // eight, eight, size).astype(BF16)
            out_ref[k * step // eight : (k + 1) * step // eight, :, at : at + size] = total


def total_body(share_ref, proj_ref, step_ref, out_ref):
    groups = share_ref.shape[0]
    inner = out_ref.shape[1]
    width = proj_ref.shape[1]
    heads = step_ref.shape[1]
    for k in range(share_ref.shape[2] // LANES):
        lanes = slice(k * LANES, (k + 1) * LANES)
        parts = [share_ref[g, :, lanes].astype(F32) for g in range(groups)]
        while len(parts) > 1:
            parts = [a + b for a, b in zip(parts[::2], parts[1::2])]
        at = k * LANES
        if at < inner:
            out_ref[:, lanes] = parts[0]
        elif at < inner + width:
            proj_ref[:, at - inner : at - inner + LANES] = parts[0]
        else:
            step_ref[...] = parts[0][:, :heads]


def exchange(array, axis):
    return lax.all_to_all(array, axis, split_axis=0, concat_axis=0, tiled=True)


def on_device(
    activations,
    in_proj,
    step_proj,
    step_bias,
    decay_rates,
    conv_kernel,
    conv_bias,
    skip_gain,
    norm_gain,
    out_proj,
    out_cotangent,
):
    frame_count, row_count, col_count, model_width = activations.shape
    inner = out_proj.shape[0]
    heads = step_proj.shape[1]
    channels = conv_bias.shape[0]
    tokens = row_count * col_count
    tm_size = lax.axis_size(TM)
    own = tokens // tm_size
    frames = frame_count * tm_size
    wide = channels + LANES
    grid4 = (row_count, col_count, frame_count)
    tok4 = (tm_size, own, frame_count)
    flat = tokens * frame_count
    core = lax.axis_index(CORE).astype(jnp.int32).reshape(1, 1)
    swap_core = [(0, 1), (1, 0)]
    devices = lax.axis_size(SPACE)
    upward = [(i, i + 1) for i in range(devices - 1)]
    downward = [(b, a) for a, b in upward]

    act = activations.transpose(1, 2, 0, 3).reshape(flat, model_width)
    cot = out_cotangent.transpose(1, 2, 0, 3).reshape(flat, model_width)
    gate_proj, mix_proj = in_proj[:, :inner], in_proj[:, inner:]
    kernel9 = conv_kernel.reshape(9, channels)
    bias1 = conv_bias.reshape(1, channels)
    both = wide + 2 * inner

    mixed = dot_nn(act, mix_proj).astype(BF16).reshape(*grid4, channels)
    low = lax.ppermute(mixed[row_count - 1], SPACE, upward)
    high = lax.ppermute(mixed[0], SPACE, downward)
    send, slope = call(
        conv_body,
        (shape_of((*grid4, channels + 2 * model_width), BF16), shape_of((*grid4, channels), F32)),
        low,
        mixed,
        high,
        kernel9,
        bias1,
        act.reshape(*grid4, model_width),
        cot.reshape(*grid4, model_width),
    )
    moved = exchange(send.reshape(tokens, frame_count, -1), TM).reshape(*tok4, -1)
    half = shape_of((model_width, flat), BF16)
    mine, other = call(turn_body, (half, half), core, cot, act, special={0: SMEM})
    theirs = lax.ppermute(other, CORE, swap_core)

    square = pltpu.VMEM((own, heads // 2, frames, 2 * frames), F32)
    d_moved, norm_part, small_part = call(
        rollout_body,
        (
            shape_of((*tok4, both), BF16),
            shape_of((1, inner), F32),
            shape_of((3, heads), F32),
        ),
        moved,
        decay_rates.reshape(1, heads),
        jnp.repeat(skip_gain, inner // heads).reshape(1, inner),
        norm_gain.reshape(1, inner),
        step_proj,
        step_bias.reshape(1, heads),
        in_proj,
        out_proj,
        special={6: ANY, 7: ANY},
        flops=1 << 29,
        scratch=(
            square,
            square,
            pltpu.VMEM((own, frames, inner), F32),
            pltpu.VMEM((own, frames, inner), BF16),
            pltpu.VMEM((frames, inner), F32),
            pltpu.VMEM((model_width, inner), BF16),
            pltpu.VMEM((inner, model_width), BF16),
            pltpu.VMEM((flat, inner), BF16),
            pltpu.VMEM((flat, inner), F32),
            pltpu.SemaphoreType.DMA((2,)),
        ),
        room=60,
    )
    home = exchange(d_moved.reshape(tokens, frame_count, both), TM)
    returned = home.reshape(*grid4, both)
    home = home.reshape(flat, both)

    d_before, sums = call(
        conv_grad_body,
        (
            shape_of((*grid4, channels), BF16),
            shape_of((16, channels), F32),
        ),
        returned,
        slope,
        low,
        mixed,
        high,
        norm_part,
        small_part,
    )
    d_low = lax.ppermute(d_before[row_count - 1], SPACE, upward)
    d_high = lax.ppermute(d_before[0], SPACE, downward)
    home2 = lax.ppermute(home, CORE, swap_core)
    late = call(
        conv_spread_body, shape_of((*grid4, wide), BF16), d_low, d_high, returned, slope, kernel9
    ).reshape(flat, wide)
    late2 = lax.ppermute(late, CORE, swap_core)
    product = call(
        outer_body,
        shape_of((model_width // 16, 8, both), BF16),
        mine,
        theirs,
        home,
        home2,
        late,
        late2,
        flops=4 * model_width // 2 * both * flat,
    )
    shares = exchange(product, CHIPS)

    sums = sums + lax.ppermute(sums, CORE, swap_core)
    for axis in (("tm_1",), ("space_1",), ("tm_0", "space_0")):
        size = lax.axis_size(axis)
        turns = []
        for k in range(1, size):
            route = [(i, (i + k) % size) for i in range(size)]
            turns.append(lax.ppermute(sums, axis, route))
        sums = (sums + turns[1]) + (turns[0] + turns[2])
    normed = home[:, wide : wide + inner]
    d_gate = home[:, wide + inner :]
    layer = dot_nn(normed, out_proj).astype(BF16)
    grad_input = (
        dot_nt(late[:, :channels], mix_proj)
        + dot_nt(late[:, channels : channels + heads], step_proj)
        + dot_nt(d_gate, gate_proj)
    ).astype(BF16)
    layer_out = layer.reshape(*grid4, model_width).transpose(2, 0, 1, 3)
    grad_input = grad_input.reshape(*grid4, model_width).transpose(2, 0, 1, 3)

    grad_in_proj, grad_step_proj, grad_out_proj_t = call(
        total_body,
        (
            shape_of((8, inner + channels), F32),
            shape_of((8, heads), F32),
            shape_of((8, inner), F32),
        ),
        shares,
    )
    return (
        layer_out,
        grad_input,
        grad_in_proj,
        grad_step_proj,
        grad_out_proj_t,
        sums[:9].reshape(3, 3, channels),
        sums[9],
        sums[11, :heads],
        sums[11, LANES : LANES + heads],
        sums[11, 2 * LANES : 2 * LANES + heads],
        sums[10, :inner],
    )


def solution(mesh):
    torus = Mesh(
        mesh.devices.reshape(2, 4, 2, 4, 2), ("tm_0", "tm_1", "space_0", "space_1", "space_2")
    )
    split = P(TM, SPACE, None, None)
    placed = (split, P(), P(), P(), P(), P(), P(), P(), P(), P(), split)
    rows = P(TM_SPACE, None)

    return jax.shard_map(
        on_device,
        mesh=torus,
        in_specs=placed,
        out_specs=(split, split, rows, rows, rows, P(), P(), P(), P(), P(), P()),
        check_vma=False,
    )
```

time: 195 us -> 167 us (0.86)
  the two profiles are of different devices: /device:TPU:0 before, /device:TPU:2 now
where the time goes in v2:
time: 167 us; the launch traced here: 166 us
  waiting for transfers between devices  64.7 us (39%)
  starting transfers between devices  46.6 us (28%)
  blocking collectives  19.9 us (12%)
  Pallas kernels  15.2 us (9%)
  local copies, waits for them, and re-layouts  10.5 us (6%)
  matrix products  7.94 us (5%)
    ppermute x9, waiting for transfers between devices, on_device(): turns.append(lax.ppermute(sums, axis, route))  49.1 us
    all_to_all x2, starting transfers between devices, exchange(): return lax.all_to_all(array, axis, split_axis=0, concat_axis=0, tiled=True)  22 us
    all_to_all x1, blocking collectives, exchange(): return lax.all_to_all(array, axis, split_axis=0, concat_axis=0, tiled=True)  19.9 us
    pallas_call x7, Pallas kernels, call(): pl.pallas_call(body, out_shape=out_shape, in_specs=specs, out_specs=outs,...  15.2 us
    ppermute x9, starting transfers between devices, on_device(): turns.append(lax.ppermute(sums, axis, route))  12.4 us
    all_to_all x2, waiting for transfers between devices, exchange(): return lax.all_to_all(array, axis, split_axis=0, concat_axis=0, tiled=True)  12.4 us
    unnamed x27, local copies, waits for them, and re-layouts  6.18 us
    dot_general x3, matrix products, dot_nt(): lax.dot_general(a, b, (((1,), (1,)), ((), ())), precision=precision, pref...  5.31 us
  transfers between devices with their start and end apart: 19, of which 11 were waited for; matrix products, arithmetic and copies ran while one was open for 7% of the time, Pallas kernels for 1%

profile of v2, /device:TPU:2, one launch (start us, length us, event | category | flops | bytes accessed | tf_op | source)
XLA Modules:
  0.0 165.8 jit_solution(17410762765377424863)
XLA Ops:
  0.7 1.1 copy.33
  1.8 2.2 %convolution_convert_fusion = bf16[128,1152]{1,0:T(8,128)(2,1)S(1)} fusion(bf16[128,1024]{1,0:T(8,128)(2,1)S(1)} %bitcast.57, bf16[1024,2176]{1,0:T(8,128)(2,1)} %in_proj_ref.1), kind=kOutput, calls=%fused_computation | convolution fusion | flops 302137344 | bytes 2916352 | tf_op jit(solution)/shard_map/dot_general | solution.py:62
  4.1 1.3 collective-permute-start.1
  5.4 3.0 %collective-permute-start = (bf16[8,8,1152]{2,1,0:T(8,128)(2,1)S(1)}, bf16[8,8,1152]{2,1,0:T(8,128)(2,1)S(1)}, u32[]{:S(2)}, u32[]{:S(2)}) collective-permute-start(bf16[8,8,1152]{2,1,0:T(8,128)(2,1)S(1)} %get-tuple-element.38), channel_id=1, source_target_pairs={{0,1},{1,2},{2,3},{3,4},{4,5},{5,6},{6,7},{7,8},{8,9},{9,10},{10,1... | collective-permute-start | bytes 442376 | tf_op jit(solution)/shard_map/ppermute | solution.py:481
  8.7 0.7 collective-permute-done.low_ref
  9.4 1.7 shard_map.194
  11.1 8.1 %all-to-all-start = ((bf16[16,8,3200]{2,1,0:T(8,128)(2,1)}), bf16[16,8,3200]{2,1,0:T(8,128)(2,1)S(1)}, u32[]{:S(2)}, u32[]{:S(2)}) async-start(bf16[16,8,3200]{2,1,0:T(8,128)(2,1)} %bitcast.6), calls=%async_computation | async-start | bytes 1638400 | tf_op jit(solution)/shard_map/all_to_all | solution.py:439
  19.3 0.7 reshape_reshape.3.skip_ref
  19.9 0.8 copy.24.step_proj_ref
  20.8 12.4 %all-to-all-done = bf16[16,8,3200]{2,1,0:T(8,128)(2,1)S(1)} async-done(((bf16[16,8,3200]{2,1,0:T(8,128)(2,1)}), bf16[16,8,3200]{2,1,0:T(8,128)(2,1)S(1)}, u32[]{:S(2)}, u32[]{:S(2)}) %all-to-all-start) | async-done | bytes 819232 | tf_op jit(solution)/shard_map/all_to_all | solution.py:439
  33.2 0.9 copy-done.6
  34.0 8.1 %shard_map.195 = (bf16[8,2,8,3328]{3,2,1,0:T(8,128)(2,1)}, f32[1,1024]{1,0:T(1,128)}, f32[3,16]{1,0:T(4,128)}) custom-call(bf16[8,2,8,3200]{3,2,1,0:T(8,128)(2,1)} %bitcast.62, f32[1,16]{1,0:T(1,128)} %bitcast.69, f32[1,1024]{1,0:T(1,128)} %reshape_reshape.3.skip_ref, f32[1,1024]{1,0:T(1,128)} %bitcast.67, bf16[1024,16]{1,0:T(8,128)(2,1)} %copy.24.step_proj_ref, ...), custom_call_target="tpu_custom_call" | custom-call | flops 536870912 | bytes 8270144 | tf_op jit(solution)/shard_map/pallas_call | solution.py:38
  42.1 19.9 %all_to_all.15 = bf16[16,8,3328]{2,1,0:T(8,128)(2,1)S(1)} all-to-all(bf16[16,8,3328]{2,1,0:T(8,128)(2,1)} %bitcast.65), channel_id=1, replica_groups=mesh['tm_0'=2,'tm_1'=4,'space_0'=2,'space_1'=4,'space_2'=2] {'tm_0','tm_1'}, dimensions={0} | all-to-all | bytes 1703936 | tf_op jit(solution)/shard_map/all_to_all | solution.py:439
  62.0 0.7 copy-done.3
  62.7 0.7 copy-done.4
  63.3 0.6 shard_map.196
  64.0 1.3 collective-permute-start.3
  65.3 3.0 %collective-permute-start.2 = (bf16[8,8,1152]{2,1,0:T(8,128)(2,1)S(1)}, bf16[8,8,1152]{2,1,0:T(8,128)(2,1)S(1)}, u32[]{:S(2)}, u32[]{:S(2)}) collective-permute-start(bf16[8,8,1152]{2,1,0:T(8,128)(2,1)S(1)} %get-tuple-element.36), channel_id=1, source_target_pairs={{0,1},{1,2},{2,3},{3,4},{4,5},{5,6},{6,7},{7,8},{8,9},{9,10},{10,1... | collective-permute-start | bytes 442376 | tf_op jit(solution)/shard_map/ppermute | solution.py:549
  68.4 1.0 collective-permute-done.2.low_ref
  69.4 0.5 shard_map.197
  69.8 3.4 %collective-permute-start.6 = (bf16[128,1280]{1,0:T(8,128)(2,1)S(1)}, bf16[128,1280]{1,0:T(8,128)(2,1)S(1)}, u32[]{:S(2)}, u32[]{:S(2)}) collective-permute-start(bf16[128,1280]{1,0:T(8,128)(2,1)S(1)} %bitcast.51), channel_id=1, source_target_pairs={{0,1},{1,0},{2,3},{3,2},{4,5},{5,4},{6,7},{7,6},{8,9},{9,8},{10,11... | collective-permute-start | bytes 983048 | tf_op jit(solution)/shard_map/ppermute | solution.py:555
  73.2 0.2 shard_map.198
  73.5 1.5 collective-permute-done.4.left2_ref
  75.1 1.1 shard_map.199
  76.1 1.7 %copy-done = bf16[64,8,3328]{2,1,0:T(8,128)(2,1)} copy-done((bf16[64,8,3328]{2,1,0:T(8,128)(2,1)}, bf16[64,8,3328]{2,1,0:T(8,128)(2,1)S(1)}, u32[]{:S(2)}) %copy-start) | copy-done | bytes 3407896
  77.9 13.8 %all-to-all-start.2 = ((bf16[64,8,3328]{2,1,0:T(8,128)(2,1)}), bf16[64,8,3328]{2,1,0:T(8,128)(2,1)}, u32[]{:S(2)}, u32[]{:S(2)}) async-start(bf16[64,8,3328]{2,1,0:T(8,128)(2,1)} %copy-done), calls=%async_computation.2 | async-start | bytes 6815744 | tf_op jit(solution)/shard_map/all_to_all | solution.py:439
  91.8 2.5 %fusion = f32[128,1024]{1,0:T(8,128)S(1)} fusion(bf16[1024,2176]{1,0:T(8,128)(2,1)} %in_proj_ref.1, bf16[128,3328]{1,0:T(8,128)(2,1)S(1)} %bitcast.49), kind=kOutput, calls=%fused_computation.1 | convolution fusion | flops 268435456 | bytes 2883584 | tf_op jit(solution)/shard_map/dot_general | solution.py:50
  94.4 0.6 collective-permute-start.10
  95.0 1.5 collective-permute-start.9
  96.5 3.3 %collective-permute-start.8 = (f32[16,1152]{1,0:T(8,128)S(1)}, f32[16,1152]{1,0:T(8,128)S(1)}, u32[]{:S(2)}, u32[]{:S(2)}) collective-permute-start(f32[16,1152]{1,0:T(8,128)S(1)} %add.38), channel_id=1, source_target_pairs={{0,32},{16,48},{32,0},{48,16},{1,33},{17,49},{33,1},{49,17},{2,34}... | collective-permute-start | bytes 221192 | tf_op jit(solution)/shard_map/ppermute | solution.py:575
  99.8 0.4 convolution_convert_fusion.1
  100.3 30.2 %collective-permute-done.10 = f32[16,1152]{1,0:T(8,128)S(1)} collective-permute-done((f32[16,1152]{1,0:T(8,128)S(1)}, f32[16,1152]{1,0:T(8,128)S(1)}, u32[]{:S(2)}, u32[]{:S(2)}) %collective-permute-start.10) | collective-permute-done | bytes 73760 | tf_op jit(solution)/shard_map/ppermute | solution.py:575
  130.4 9.2 %collective-permute-done.9 = f32[16,1152]{1,0:T(8,128)S(1)} collective-permute-done((f32[16,1152]{1,0:T(8,128)S(1)}, f32[16,1152]{1,0:T(8,128)S(1)}, u32[]{:S(2)}, u32[]{:S(2)}) %collective-permute-start.9) | collective-permute-done | bytes 73760 | tf_op jit(solution)/shard_map/ppermute | solution.py:575
  139.7 4.5 %collective-permute-done.8 = f32[16,1152]{1,0:T(8,128)S(1)} collective-permute-done((f32[16,1152]{1,0:T(8,128)S(1)}, f32[16,1152]{1,0:T(8,128)S(1)}, u32[]{:S(2)}, u32[]{:S(2)}) %collective-permute-start.8) | collective-permute-done | bytes 73760 | tf_op jit(solution)/shard_map/ppermute | solution.py:575
  144.2 0.3 collective-permute-start.13
  144.4 2.0 %collective-permute-start.12 = (f32[16,1152]{1,0:T(8,128)S(1)}, f32[16,1152]{1,0:T(8,128)S(1)}, u32[]{:S(2)}, u32[]{:S(2)}) collective-permute-start(f32[16,1152]{1,0:T(8,128)S(1)} %add_add_fusion.2), channel_id=1, source_target_pairs={{0,2},{2,4},{4,6},{6,0},{1,3},{3,5},{5,7},{7,1},{8,10},{10,12},{12... | collective-permute-start | bytes 221192 | tf_op jit(solution)/shard_map/ppermute | solution.py:575
  146.7 2.6 %fusion.11 = bf16[128,1024]{1,0:T(8,128)(2,1)S(1)} fusion(f32[128,1024]{1,0:T(8,128)S(1)} %fusion, f32[128,1024]{1,0:T(8,128)S(1)} %fusion.17, bf16[1024,2176]{1,0:T(8,128)(2,1)} %in_proj_ref.1, bf16[128,1280]{1,0:T(8,128)(2,1)S(1)} %bitcast.54), kind=kOutput, calls=%fused_computation.8 | convolution fusion | flops 302383104 | bytes 3964928 | tf_op jit(solution)/shard_map/dot_general | solution.py:50
  149.4 1.1 collective-permute-done.12
  150.5 1.8 %collective-permute-done.11 = f32[16,1152]{1,0:T(8,128)S(1)} collective-permute-done((f32[16,1152]{1,0:T(8,128)S(1)}, f32[16,1152]{1,0:T(8,128)S(1)}, u32[]{:S(2)}, u32[]{:S(2)}) %collective-permute-start.11) | collective-permute-done | bytes 73760 | tf_op jit(solution)/shard_map/ppermute | solution.py:575
  152.4 2.0 %collective-permute-start.15 = (f32[16,1152]{1,0:T(8,128)S(1)}, f32[16,1152]{1,0:T(8,128)S(1)}, u32[]{:S(2)}, u32[]{:S(2)}) collective-permute-start(f32[16,1152]{1,0:T(8,128)S(1)} %add_add_fusion.1), channel_id=1, source_target_pairs={{0,8},{8,64},{64,72},{72,0},{1,9},{9,65},{65,73},{73,1},{2,10},{10... | collective-permute-start | bytes 221192 | tf_op jit(solution)/shard_map/ppermute | solution.py:575
  154.4 2.7 %collective-permute-start.14 = (f32[16,1152]{1,0:T(8,128)S(1)}, f32[16,1152]{1,0:T(8,128)S(1)}, u32[]{:S(2)}, u32[]{:S(2)}) collective-permute-start(f32[16,1152]{1,0:T(8,128)S(1)} %add_add_fusion.1), channel_id=1, source_target_pairs={{0,64},{8,72},{64,0},{72,8},{1,65},{9,73},{65,1},{73,9},{2,66},{10... | collective-permute-start | bytes 221192 | tf_op jit(solution)/shard_map/ppermute | solution.py:575
  157.1 1.1 copy_bitcast_fusion
  158.2 2.1 %collective-permute-done.14 = f32[16,1152]{1,0:T(8,128)S(1)} collective-permute-done((f32[16,1152]{1,0:T(8,128)S(1)}, f32[16,1152]{1,0:T(8,128)S(1)}, u32[]{:S(2)}, u32[]{:S(2)}) %collective-permute-start.14) | collective-permute-done | bytes 73760 | tf_op jit(solution)/shard_map/ppermute | solution.py:575
  160.3 0.6 slice.77
  160.9 0.6 reshape.97
  161.6 0.6 slice_reduce_fusion
  162.2 0.5 slice_bitcast_fusion.4
  162.7 3.1 %shard_map.200 = (f32[8,2176]{1,0:T(8,128)}, f32[8,16]{1,0:T(8,128)}, f32[8,1024]{1,0:T(8,128)}) custom-call(bf16[64,8,3328]{2,1,0:T(8,128)(2,1)} %all-to-all-done.2.share_ref), custom_call_target="tpu_custom_call" | custom-call | flops 1048576 | bytes 3510784 | tf_op jit(solution)/shard_map/pallas_call | solution.py:38
  (45 shorter events, 1.0 us)
Async XLA Ops:
  0.6 7.8 %copy-start.10 = (f32[1152]{0:T(1024)S(1)}, f32[1152]{0:T(1024)}, u32[]{:S(2)}) copy-start(f32[1152]{0:T(1024)} %param.17) | copy-start | bytes 13828
  0.7 7.8 %copy-start.9 = (f32[3,3,1152]{2,1,0:T(4,128)S(1)}, f32[3,3,1152]{2,1,0:T(4,128)}, u32[]{:S(2)}) copy-start(f32[3,3,1152]{2,1,0:T(4,128)} %param.16) | copy-start | bytes 124420
  0.7 7.8 %copy-start.7 = (bf16[8,2,8,1024]{3,2,1,0:T(8,128)(2,1)S(1)}, bf16[8,2,8,1024]{3,2,1,0:T(8,128)(2,1)}, u32[]{:S(2)}) copy-start(bf16[8,2,8,1024]{3,2,1,0:T(8,128)(2,1)} %param.21) | copy-start | bytes 786436
  4.0 15.2 %copy-start.11 = (f32[16]{0:T(128)S(1)}, f32[16]{0:T(128)}, u32[]{:S(2)}) copy-start(f32[16]{0:T(128)} %param.18) | copy-start | bytes 196
  4.0 15.9 %copy-start.8 = (bf16[1024,16]{0,1:T(8,128)(2,1)S(1)}, bf16[1024,16]{0,1:T(8,128)(2,1)}, u32[]{:S(2)}) copy-start(bf16[1024,16]{0,1:T(8,128)(2,1)} %param.13) | copy-start | bytes 98308
  4.1 4.6 %collective-permute-start.1 = (bf16[8,8,1152]{2,1,0:T(8,128)(2,1)S(1)}, bf16[8,8,1152]{2,1,0:T(8,128)(2,1)S(1)}, u32[]{:S(2)}, u32[]{:S(2)}) collective-permute-start(bf16[8,8,1152]{2,1,0:T(8,128)(2,1)S(1)} %get-tuple-element.37), channel_id=1, source_target_pairs={{1,0},{2,1},{3,2},{4,3},{5,4},{6,5},{7,6},{8,7},{9,8},{10,9},{11,1... | collective-permute-start | bytes 442376 | tf_op jit(solution)/shard_map/ppermute | solution.py:482
  5.4 4.0 %collective-permute-start = (bf16[8,8,1152]{2,1,0:T(8,128)(2,1)S(1)}, bf16[8,8,1152]{2,1,0:T(8,128)(2,1)S(1)}, u32[]{:S(2)}, u32[]{:S(2)}) collective-permute-start(bf16[8,8,1152]{2,1,0:T(8,128)(2,1)S(1)} %get-tuple-element.38), channel_id=1, source_target_pairs={{0,1},{1,2},{2,3},{3,4},{4,5},{5,6},{6,7},{7,8},{8,9},{9,10},{10,1... | collective-permute-start | bytes 442376 | tf_op jit(solution)/shard_map/ppermute | solution.py:481
  11.1 22.1 %all-to-all-start = ((bf16[16,8,3200]{2,1,0:T(8,128)(2,1)}), bf16[16,8,3200]{2,1,0:T(8,128)(2,1)S(1)}, u32[]{:S(2)}, u32[]{:S(2)}) async-start(bf16[16,8,3200]{2,1,0:T(8,128)(2,1)} %bitcast.6), calls=%async_computation | async-start | bytes 1638400 | tf_op jit(solution)/shard_map/all_to_all | solution.py:439
  33.2 0.9 copy-start.6
  62.0 13.1 %collective-permute-start.5 = (bf16[128,3328]{1,0:T(8,128)(2,1)S(1)}, bf16[128,3328]{1,0:T(8,128)(2,1)S(1)}, u32[]{:S(2)}, u32[]{:S(2)}) collective-permute-start(bf16[128,3328]{1,0:T(8,128)(2,1)S(1)} %bitcast.45), channel_id=1, source_target_pairs={{0,1},{1,0},{2,3},{3,2},{4,5},{5,4},{6,7},{7,6},{8,9},{9,8},{10,11... | collective-permute-start | bytes 2555912 | tf_op jit(solution)/shard_map/ppermute | solution.py:551
  62.0 0.7 copy-start.3
  62.7 0.7 copy-start.4
  64.0 5.8 %copy-start.1 = (f32[16,1152]{1,0:T(8,128)}, f32[16,1152]{1,0:T(8,128)S(1)}, u32[]{:S(2)}) copy-start(f32[16,1152]{1,0:T(8,128)S(1)} %get-tuple-element.34) | copy-start | bytes 221188
  64.0 4.4 %collective-permute-start.3 = (bf16[8,8,1152]{2,1,0:T(8,128)(2,1)S(1)}, bf16[8,8,1152]{2,1,0:T(8,128)(2,1)S(1)}, u32[]{:S(2)}, u32[]{:S(2)}) collective-permute-start(bf16[8,8,1152]{2,1,0:T(8,128)(2,1)S(1)} %get-tuple-element.35), channel_id=1, source_target_pairs={{1,0},{2,1},{3,2},{4,3},{5,4},{6,5},{7,6},{8,7},{9,8},{10,9},{11,1... | collective-permute-start | bytes 442376 | tf_op jit(solution)/shard_map/ppermute | solution.py:550
  65.3 4.0 %collective-permute-start.2 = (bf16[8,8,1152]{2,1,0:T(8,128)(2,1)S(1)}, bf16[8,8,1152]{2,1,0:T(8,128)(2,1)S(1)}, u32[]{:S(2)}, u32[]{:S(2)}) collective-permute-start(bf16[8,8,1152]{2,1,0:T(8,128)(2,1)S(1)} %get-tuple-element.36), channel_id=1, source_target_pairs={{0,1},{1,2},{2,3},{3,4},{4,5},{5,6},{6,7},{7,8},{8,9},{9,10},{10,1... | collective-permute-start | bytes 442376 | tf_op jit(solution)/shard_map/ppermute | solution.py:549
  69.8 5.2 %collective-permute-start.6 = (bf16[128,1280]{1,0:T(8,128)(2,1)S(1)}, bf16[128,1280]{1,0:T(8,128)(2,1)S(1)}, u32[]{:S(2)}, u32[]{:S(2)}) collective-permute-start(bf16[128,1280]{1,0:T(8,128)(2,1)S(1)} %bitcast.51), channel_id=1, source_target_pairs={{0,1},{1,0},{2,3},{3,2},{4,5},{5,4},{6,7},{7,6},{8,9},{9,8},{10,11... | collective-permute-start | bytes 983048 | tf_op jit(solution)/shard_map/ppermute | solution.py:555
  73.4 1.6 collective-permute-start.4
  76.1 1.8 %copy-start = (bf16[64,8,3328]{2,1,0:T(8,128)(2,1)}, bf16[64,8,3328]{2,1,0:T(8,128)(2,1)S(1)}, u32[]{:S(2)}) copy-start(bf16[64,8,3328]{2,1,0:T(8,128)(2,1)S(1)} %shard_map.199) | copy-start | bytes 10223620
  77.9 13.9 %copy-start.2 = (f32[16,1152]{1,0:T(8,128)S(1)}, f32[16,1152]{1,0:T(8,128)}, u32[]{:S(2)}) copy-start(f32[16,1152]{1,0:T(8,128)} %copy-done.1) | copy-start | bytes 221188
  77.9 84.8 %all-to-all-start.2 = ((bf16[64,8,3328]{2,1,0:T(8,128)(2,1)}), bf16[64,8,3328]{2,1,0:T(8,128)(2,1)}, u32[]{:S(2)}, u32[]{:S(2)}) async-start(bf16[64,8,3328]{2,1,0:T(8,128)(2,1)} %copy-done), calls=%async_computation.2 | async-start | bytes 6815744 | tf_op jit(solution)/shard_map/all_to_all | solution.py:439
  91.7 8.1 %copy-start.5 = (bf16[1024,1024]{1,0:T(8,128)(2,1)S(1)}, bf16[1024,1024]{1,0:T(8,128)(2,1)}, u32[]{:S(2)}) copy-start(bf16[1024,1024]{1,0:T(8,128)(2,1)} %out_proj_ref.1) | copy-start | bytes 6291460
  91.7 2.6 %collective-permute-start.7 = (f32[16,1152]{1,0:T(8,128)S(1)}, f32[16,1152]{1,0:T(8,128)S(1)}, u32[]{:S(2)}, u32[]{:S(2)}) collective-permute-start(f32[16,1152]{1,0:T(8,128)S(1)} %copy-done.2), channel_id=1, source_target_pairs={{0,1},{1,0},{2,3},{3,2},{4,5},{5,4},{6,7},{7,6},{8,9},{9,8},{10,11... | collective-permute-start | bytes 221192 | tf_op jit(solution)/shard_map/ppermute | solution.py:569
  94.4 36.0 %collective-permute-start.10 = (f32[16,1152]{1,0:T(8,128)S(1)}, f32[16,1152]{1,0:T(8,128)S(1)}, u32[]{:S(2)}, u32[]{:S(2)}) collective-permute-start(f32[16,1152]{1,0:T(8,128)S(1)} %add.38), channel_id=1, source_target_pairs={{0,48},{16,0},{32,16},{48,32},{1,49},{17,1},{33,17},{49,33},{2,50}... | collective-permute-start | bytes 221192 | tf_op jit(solution)/shard_map/ppermute | solution.py:575
  95.0 44.7 %collective-permute-start.9 = (f32[16,1152]{1,0:T(8,128)S(1)}, f32[16,1152]{1,0:T(8,128)S(1)}, u32[]{:S(2)}, u32[]{:S(2)}) collective-permute-start(f32[16,1152]{1,0:T(8,128)S(1)} %add.38), channel_id=1, source_target_pairs={{0,16},{16,32},{32,48},{48,0},{1,17},{17,33},{33,49},{49,1},{2,18}... | collective-permute-start | bytes 221192 | tf_op jit(solution)/shard_map/ppermute | solution.py:575
  96.5 47.7 %collective-permute-start.8 = (f32[16,1152]{1,0:T(8,128)S(1)}, f32[16,1152]{1,0:T(8,128)S(1)}, u32[]{:S(2)}, u32[]{:S(2)}) collective-permute-start(f32[16,1152]{1,0:T(8,128)S(1)} %add.38), channel_id=1, source_target_pairs={{0,32},{16,48},{32,0},{48,16},{1,33},{17,49},{33,1},{49,17},{2,34}... | collective-permute-start | bytes 221192 | tf_op jit(solution)/shard_map/ppermute | solution.py:575
  144.2 5.2 %collective-permute-start.13 = (f32[16,1152]{1,0:T(8,128)S(1)}, f32[16,1152]{1,0:T(8,128)S(1)}, u32[]{:S(2)}, u32[]{:S(2)}) collective-permute-start(f32[16,1152]{1,0:T(8,128)S(1)} %add_add_fusion.2), channel_id=1, source_target_pairs={{0,6},{2,0},{4,2},{6,4},{1,7},{3,1},{5,3},{7,5},{8,14},{10,8},{12,... | collective-permute-start | bytes 221192 | tf_op jit(solution)/shard_map/ppermute | solution.py:575
  144.4 6.0 %collective-permute-start.12 = (f32[16,1152]{1,0:T(8,128)S(1)}, f32[16,1152]{1,0:T(8,128)S(1)}, u32[]{:S(2)}, u32[]{:S(2)}) collective-permute-start(f32[16,1152]{1,0:T(8,128)S(1)} %add_add_fusion.2), channel_id=1, source_target_pairs={{0,2},{2,4},{4,6},{6,0},{1,3},{3,5},{5,7},{7,1},{8,10},{10,12},{12... | collective-permute-start | bytes 221192 | tf_op jit(solution)/shard_map/ppermute | solution.py:575
  146.5 5.9 %collective-permute-start.11 = (f32[16,1152]{1,0:T(8,128)S(1)}, f32[16,1152]{1,0:T(8,128)S(1)}, u32[]{:S(2)}, u32[]{:S(2)}) collective-permute-start(f32[16,1152]{1,0:T(8,128)S(1)} %add_add_fusion.2), channel_id=1, source_target_pairs={{0,4},{2,6},{4,0},{6,2},{1,5},{3,7},{5,1},{7,3},{8,12},{10,14},{12... | collective-permute-start | bytes 221192 | tf_op jit(solution)/shard_map/ppermute | solution.py:575
  152.3 5.8 %collective-permute-start.16 = (f32[16,1152]{1,0:T(8,128)S(1)}, f32[16,1152]{1,0:T(8,128)S(1)}, u32[]{:S(2)}, u32[]{:S(2)}) collective-permute-start(f32[16,1152]{1,0:T(8,128)S(1)} %add_add_fusion.1), channel_id=1, source_target_pairs={{0,72},{8,0},{64,8},{72,64},{1,73},{9,1},{65,9},{73,65},{2,74},{10... | collective-permute-start | bytes 221192 | tf_op jit(solution)/shard_map/ppermute | solution.py:575
  152.4 5.8 %collective-permute-start.15 = (f32[16,1152]{1,0:T(8,128)S(1)}, f32[16,1152]{1,0:T(8,128)S(1)}, u32[]{:S(2)}, u32[]{:S(2)}) collective-permute-start(f32[16,1152]{1,0:T(8,128)S(1)} %add_add_fusion.1), channel_id=1, source_target_pairs={{0,8},{8,64},{64,72},{72,0},{1,9},{9,65},{65,73},{73,1},{2,10},{10... | collective-permute-start | bytes 221192 | tf_op jit(solution)/shard_map/ppermute | solution.py:575
  154.4 5.9 %collective-permute-start.14 = (f32[16,1152]{1,0:T(8,128)S(1)}, f32[16,1152]{1,0:T(8,128)S(1)}, u32[]{:S(2)}, u32[]{:S(2)}) collective-permute-start(f32[16,1152]{1,0:T(8,128)S(1)} %add_add_fusion.1), channel_id=1, source_target_pairs={{0,64},{8,72},{64,0},{72,8},{1,65},{9,73},{65,1},{73,9},{2,66},{10... | collective-permute-start | bytes 221192 | tf_op jit(solution)/shard_map/ppermute | solution.py:575
